TPU v7x, 32 devices: a whole 2x2x4 slice. The times are simulated.
32 devices in a mesh: seq: 8 (over z, y), head: 4 (over x, core).
Axes of the slice: x: 2, y: 2, z: 4, core: 2. Of those that a mesh axis runs over, the one named last changes fastest.
Arguments:
- xs: bfloat16 [2048, 8192], P('seq', 'head'), may hold values from -6 to 6
- gate_z: bfloat16 [2048, 8192], P('seq', 'head'), may hold values from -400 to 400
- b_in: bfloat16 [2048, 1024], P('seq', 'head'), may hold values from -6 to 6
- c_in: bfloat16 [2048, 1024], P('seq', 'head'), may hold values from -6 to 6
- dt: float32 [2048, 128], P('seq', 'head'), may hold values from 0 to 0.07
- log_decay: float32 [2048, 128], P('seq', 'head'), may hold values from -0.7 to 0
- d_skip: float32 [128], P('head'), may hold values from 1 to 3
- conv_x: float32 [4, 8192], P(None, 'head'), may hold values from -3 to 3
- conv_b: float32 [4, 1024], P(None, 'head'), may hold values from -3 to 3
- conv_c: float32 [4, 1024], P(None, 'head'), may hold values from -3 to 3
- norm_gain: float32 [8192], P('head'), may hold values from 0.1 to 1.9
- doc_lengths: int32 [4], replicated, may hold values from 1 to 1024, 2048 in all
Outputs:
- mixed: bfloat16 [2048, 8192], P('seq', 'head')
Inputs may be any that keep to these rules, and one draw needn't show every extreme that they name: `doc_lengths`: the longest document has exactly 1024 tokens; they add up to 2048.
All inputs are finite; a program needn't handle non-finite values.
Results may differ from a plain program's by a relative error of at most 0.0045.
Values may be sent and summed in bfloat16 or wider, within the bound.
A program may use at most 64 MiB of HBM per device.

v0:
```python
import functools

import jax
import jax.numpy as jnp
from jax import lax
from jax.experimental import pallas as pl
from jax.experimental.pallas import tpu as pltpu
from jax.sharding import PartitionSpec as P

HEAD_DIM = 64
STATE = 128
BLOCK = 128
LANES = 128
WIDE = 256
HALO = 16
SUBS = 2
norm_epsilon = 1e-05

MESH = pl.DeviceIdType.MESH
f32 = jnp.float32
bf16 = jnp.bfloat16


def silu(v):
    return v / (1.0 + jnp.exp(-v))


def split(v):
    high = v.astype(bf16)
    rest = v - high.astype(f32)
    middle = rest.astype(bf16)
    low = (rest - middle.astype(f32)).astype(bf16)
    parts = [high.astype(f32), middle.astype(f32), low.astype(f32)]
    width = LANES - 3 * v.shape[1]
    if width:
        parts.append(jnp.zeros((v.shape[0], width), f32))
    return jnp.concatenate(parts, axis=1).astype(bf16)


def dot(a, b):
    return jnp.dot(a, b, preferred_element_type=f32)


def kernel(
    seq_size,
    head_size,
    lengths_ref,
    xs_hbm,
    z_hbm,
    b_ref,
    c_ref,
    dt_ref,
    decay_ref,
    skip_ref,
    conv_x_ref,
    conv_b_ref,
    conv_c_ref,
    gain_ref,
    out_ref,
    xs_ref,
    z_ref,
    halo_x,
    halo_b,
    halo_c,
    own_s,
    pair_s,
    chain_out,
    chain_in,
    first_s,
    d_own,
    d_pair,
    masks,
    x_conv,
    scaled,
    c_conv,
    b_conv,
    b_turned,
    score,
    cum_turned,
    packed,
    gated,
    square,
    square_own,
    square_in,
    halo_send,
    halo_recv,
    d_send,
    d_recv,
    pair_send,
    pair_recv,
    chain_send,
    chain_recv,
    square_send,
    square_recv,
    load_sem,
):
    rows = xs_ref.shape[0]
    heads = dt_ref.shape[0]
    groups = b_ref.shape[1] // STATE
    chunks = xs_ref.shape[1] // WIDE
    per_chunk = WIDE // HEAD_DIM
    blocks = rows // BLOCK
    docs = lengths_ref.shape[0]
    k = lax.axis_index("seq")
    me = lax.axis_index("head")
    r = lax.rem(k, 2)
    partner = k + 1 - 2 * r
    has_prev = k > 0
    has_next = k + 1 < seq_size
    has_chain_in = k > 1
    has_chain_out = k + 2 < seq_size

    def halo_copies():
        pairs = ((xs_hbm, halo_x), (b_ref, halo_b), (c_ref, halo_c))
        return [
            pltpu.make_async_remote_copy(
                src_ref=source.at[pl.ds(rows - HALO, HALO)],
                dst_ref=target,
                send_sem=halo_send.at[i],
                recv_sem=halo_recv.at[i],
                device_id={"seq": k + 1},
                device_id_type=MESH,
            )
            for i, (source, target) in enumerate(pairs)
        ]

    def d_copy():
        return pltpu.make_async_remote_copy(
            src_ref=d_own,
            dst_ref=d_pair,
            send_sem=d_send,
            recv_sem=d_recv,
            device_id={"seq": partner},
            device_id_type=MESH,
        )

    def pair_copy(c, part):
        lines = pl.ds(part * (STATE // SUBS), STATE // SUBS)
        return pltpu.make_async_remote_copy(
            src_ref=own_s.at[c, lines],
            dst_ref=pair_s.at[c, lines],
            send_sem=pair_send.at[c, part],
            recv_sem=pair_recv.at[c, part],
            device_id={"seq": partner},
            device_id_type=MESH,
        )

    def chain_copy(c, part):
        lines = pl.ds(part * (STATE // SUBS), STATE // SUBS)
        return pltpu.make_async_remote_copy(
            src_ref=chain_out.at[c, lines],
            dst_ref=chain_in.at[c, lines],
            send_sem=chain_send.at[c, part],
            recv_sem=chain_recv.at[c, part],
            device_id={"seq": k + 2},
            device_id_type=MESH,
        )

    def square_copy(d):
        return pltpu.make_async_remote_copy(
            src_ref=square_own,
            dst_ref=square_in.at[d - 1],
            send_sem=square_send.at[d - 1],
            recv_sem=square_recv.at[d - 1],
            device_id={"head": lax.rem(me + d, head_size)},
            device_id_type=MESH,
        )

    load_x = pltpu.make_async_copy(xs_hbm, xs_ref, load_sem.at[0])
    load_z = pltpu.make_async_copy(z_hbm, z_ref, load_sem.at[1])
    load_x.start()

    barrier = pltpu.get_barrier_semaphore()
    for step, there in ((-1, has_prev), (1, has_next), (-2, has_chain_in), (2, has_chain_out)):

        @pl.when(there)
        def _():
            pl.semaphore_signal(
                barrier, inc=1, device_id={"seq": k + step}, device_id_type=MESH
            )

    for d in range(1, head_size):
        pl.semaphore_signal(
            barrier,
            inc=1,
            device_id={"head": lax.rem(me + d, head_size)},
            device_id_type=MESH,
        )
    expected = head_size - 1
    for there in (has_prev, has_next, has_chain_in, has_chain_out):
        expected = expected + there.astype(jnp.int32)
    @pl.when(k == 0)
    def _():
        halo_x[...] = jnp.zeros_like(halo_x)
        halo_b[...] = jnp.zeros_like(halo_b)
        halo_c[...] = jnp.zeros_like(halo_c)

    @pl.when(k < 2)
    def _():
        chain_in[...] = jnp.zeros_like(chain_in)

    starts = []
    running = jnp.int32(0)
    for j in range(docs):
        starts.append(running)
        running = running + lengths_ref[j]

    def doc_at(position):
        found = jnp.full_like(position, -1)
        for start in starts:
            found = found + jnp.where(start <= position, 1, 0)
        return found

    base = k * rows
    column = base + lax.broadcasted_iota(jnp.int32, (rows, LANES), 0)
    doc_column = doc_at(column)
    for d in range(1, 4):
        masks[d - 1] = jnp.where(doc_at(column - d) == doc_column, 1.0, 0.0).astype(f32)
    entries = [doc_at(base + b * BLOCK - 1) for b in range(blocks)]
    lasts = [doc_at(base + (b + 1) * BLOCK - 1) for b in range(blocks)]

    pl.semaphore_wait(barrier, expected)

    @pl.when(has_next)
    def _():
        for copy in halo_copies():
            copy.start()

    load_z.start()

    def turn(v):
        wide = jnp.concatenate([v, jnp.zeros((LANES - heads, rows), f32)], axis=0)
        return wide.T[:, :heads]

    dt_rows = turn(dt_ref[...])
    decay_rows = turn(decay_ref[...])
    t_index = lax.broadcasted_iota(jnp.int32, (BLOCK, BLOCK), 0)
    s_index = lax.broadcasted_iota(jnp.int32, (BLOCK, BLOCK), 1)
    lower = jnp.where(s_index <= t_index, 1.0, 0.0).astype(bf16)
    ends, enters, cums = [], [], []
    for b in range(blocks):
        here = slice(b * BLOCK, (b + 1) * BLOCK)
        parts = dot(lower, split(decay_rows[here, :]))
        cum = parts[:, :heads] + parts[:, heads : 2 * heads] + parts[:, 2 * heads : 3 * heads]
        doc = doc_column[here, :heads]
        ends.append(jnp.where(doc == lasts[b], jnp.exp(cum[BLOCK - 1 :, :] - cum), 0.0))
        enters.append(jnp.where(doc == entries[b], jnp.exp(cum), 0.0))
        cums.append(cum)
        wide = jnp.concatenate([cum, jnp.zeros((BLOCK, LANES - heads), f32)], axis=1)
        turned = wide.T
        for c in range(chunks):
            cum_turned[b, c, 0:per_chunk, :] = turned[c * per_chunk : (c + 1) * per_chunk, :]
    carry0 = enters[0][BLOCK - 1 :, :]
    carry1 = enters[1][BLOCK - 1 :, :]
    packed[0] = split(dt_rows)
    packed[1] = split(jnp.concatenate(ends, axis=0))
    packed[2] = split(jnp.concatenate([enters[0], enters[1] * carry0], axis=0))
    packed[3] = split(jnp.concatenate([enters[0], enters[1]], axis=0))
    packed[4] = split(jnp.concatenate(cums, axis=0))
    d_own[...] = split(jnp.broadcast_to(carry0 * carry1, (16, heads)))
    d_copy().start()
    few = split(
        jnp.concatenate(
            [jnp.broadcast_to(carry1, (8, heads)), jnp.broadcast_to(skip_ref[...], (8, heads))], 0
        )
    )
    packed[5, 0:16, :] = few

    def spread(c, width):
        row = lax.broadcasted_iota(jnp.int32, (LANES, per_chunk * width), 0)
        lane = lax.broadcasted_iota(jnp.int32, (LANES, per_chunk * width), 1)
        wanted = c * per_chunk + lane // width
        hit = (row == wanted) | (row == wanted + heads) | (row == wanted + 2 * heads)
        return jnp.where(hit, 1.0, 0.0).astype(bf16)

    def convolve(x, weight):
        x = x.astype(f32)
        total = weight[3:4, :] * x
        for d in range(1, 4):
            total = total + weight[3 - d : 4 - d, :] * (pltpu.roll(x, d, 0) * masks[d - 1])
        return silu(total).astype(bf16)

    def convolve_top(x, halo, weight):
        window = jnp.concatenate([halo.astype(f32), x.astype(f32)], axis=0)
        total = weight[3:4, :] * window[HALO:]
        for d in range(1, 4):
            shifted = window[HALO - d : 2 * HALO - d] * masks[d - 1, 0:HALO, :]
            total = total + weight[3 - d : 4 - d, :] * shifted
        return silu(total).astype(bf16)

    for g in range(groups):
        lanes = slice(g * STATE, (g + 1) * STATE)
        b_conv[g] = convolve(b_ref[:, lanes], conv_b_ref[:, lanes])
        c_conv[g] = convolve(c_ref[:, lanes], conv_c_ref[:, lanes])
        b_turned[g, 1] = b_conv[g, BLOCK:, :].astype(f32).T.astype(bf16)

    load_x.wait()

    def lanes_of(c, half):
        return pl.ds(pl.multiple_of(c * WIDE + half * LANES, LANES), LANES)

    def conv_step(c, _):
        for half in range(WIDE // LANES):
            lanes = lanes_of(c, half)
            x_conv[c, :, half * LANES : (half + 1) * LANES] = convolve(
                xs_ref[:, lanes], conv_x_ref[:, lanes]
            )
        return 0

    lax.fori_loop(0, chunks, conv_step, 0)

    @pl.when(has_prev)
    def _():
        for copy in halo_copies():
            copy.wait_recv()

    for g in range(groups):
        lanes = slice(g * STATE, (g + 1) * STATE)
        b_conv[g, 0:HALO, :] = convolve_top(b_ref[0:HALO, lanes], halo_b[:, lanes], conv_b_ref[:, lanes])
        c_conv[g, 0:HALO, :] = convolve_top(c_ref[0:HALO, lanes], halo_c[:, lanes], conv_c_ref[:, lanes])
        b_turned[g, 0] = b_conv[g, :BLOCK, :].astype(f32).T.astype(bf16)

    def state_step(c, _):
        g = c // (chunks // groups)
        for half in range(WIDE // LANES):
            lanes = lanes_of(c, half)
            x_conv[c, 0:HALO, half * LANES : (half + 1) * LANES] = convolve_top(
                xs_ref[0:HALO, lanes], halo_x[:, lanes], conv_x_ref[:, lanes]
            )
        x = x_conv[c]
        one_hot = spread(c, HEAD_DIM)
        product = (dot(packed[0], one_hot) * x.astype(f32)).astype(bf16)
        scaled[c] = product
        weighted = (dot(packed[1], one_hot) * product.astype(f32)).astype(bf16)
        state0 = dot(b_turned[g, 0], weighted[:BLOCK])
        state1 = dot(b_turned[g, 1], weighted[BLOCK:])
        few = dot(packed[5, 0:16, :], one_hot)
        first_s[c] = state0.astype(bf16)
        own_s[c] = (few[0:1, :] * state0 + state1).astype(bf16)
        for part in range(SUBS):
            pair_copy(c, part).start()
        return 0

    lax.fori_loop(0, chunks, state_step, 0)

    for b in range(blocks):
        here = slice(b * BLOCK, (b + 1) * BLOCK)
        doc_row = doc_at(base + b * BLOCK + lax.broadcasted_iota(jnp.int32, (8, BLOCK), 1))[0:1, :]
        allowed = (doc_column[here, :] == doc_row) & (s_index <= t_index)
        for g in range(groups):
            value = lax.dot_general(
                c_conv[g, here, :],
                b_conv[g, here, :],
                (((1,), (1,)), ((), ())),
                preferred_element_type=f32,
            )
            score[g, b] = jnp.where(allowed, value, 0.0)

    square[...] = jnp.zeros_like(square)
    d_copy().wait_recv()
    load_z.wait()
    even = r == 0

    def main_step(c, _):
        g = c // (chunks // groups)
        one_hot = spread(c, HEAD_DIM)
        decay_own = dot(d_own[...], one_hot)[0:1, :]
        decay_pair = dot(d_pair[...], one_hot)[0:1, :]
        decay_first = jnp.where(even, decay_own, decay_pair)
        decay_second = jnp.where(even, decay_pair, decay_own)
        pieces = []
        for part in range(SUBS):
            lines = pl.ds(part * (STATE // SUBS), STATE // SUBS)
            pair_copy(c, part).wait_recv()

            @pl.when(has_chain_in)
            def _():
                chain_copy(c, part).wait_recv()

            own = own_s[c, lines].astype(f32)
            other = pair_s[c, lines].astype(f32)
            before = chain_in[c, lines].astype(f32)
            middle = jnp.where(even, own, other) + decay_first * before
            after = jnp.where(even, other, own) + decay_second * middle

            @pl.when(has_chain_out)
            def _():
                chain_out[c, lines] = after.astype(bf16)
                chain_copy(c, part).start()

            pieces.append(jnp.where(even, before, middle).astype(bf16))
        entering = jnp.concatenate(pieces, axis=0)
        one_hot_wide = spread(c, BLOCK)
        lane = lax.broadcasted_iota(jnp.int32, (BLOCK, LANES), 1)
        locals_ = []
        for b in range(blocks):
            here = slice(b * BLOCK, (b + 1) * BLOCK)
            across = dot(packed[4, here, :], one_hot_wide)
            damped = score[g, b]
            pieces = []
            for j in range(per_chunk // 2):
                mixes = []
                for i in (2 * j, 2 * j + 1):
                    gap = across[:, i * BLOCK : (i + 1) * BLOCK] - cum_turned[b, c, i : i + 1, :]
                    mixes.append((damped * jnp.exp(jnp.minimum(gap, 0.0))).astype(bf16))
                values = scaled[c, here, j * LANES : (j + 1) * LANES]
                zero = jnp.zeros_like(values)
                left = jnp.where(lane < HEAD_DIM, values, zero)
                right = jnp.where(lane < HEAD_DIM, zero, values)
                pieces.append(
                    dot(jnp.concatenate(mixes, axis=1), jnp.concatenate([left, right], axis=0))
                )
            locals_.append(jnp.concatenate(pieces, axis=1))
        inner = dot(packed[3, BLOCK:, :], one_hot) * dot(c_conv[g, BLOCK:, :], first_s[c])
        few = dot(packed[5, 0:16, :], one_hot)
        total = jnp.concatenate([locals_[0], locals_[1] + inner], axis=0)
        total = total + few[8:9, :] * x_conv[c].astype(f32)
        total = total + dot(packed[2], one_hot) * dot(c_conv[g], entering)
        lanes = pl.ds(pl.multiple_of(c * WIDE, WIDE), WIDE)
        value = total * silu(z_ref[:, lanes].astype(f32))
        gated[c] = value
        power = value * value
        square[...] += power[:, :LANES] + power[:, LANES:]
        return 0

    lax.fori_loop(0, chunks, main_step, 0)

    own_square = jnp.sum(square[...].T, axis=0, keepdims=True)
    square_own[...] = jnp.broadcast_to(own_square, square_own.shape)
    for d in range(1, head_size):
        square_copy(d).start()
    for d in range(1, head_size):
        square_copy(d).wait_recv()
    total_square = square_own[...]
    for d in range(1, head_size):
        total_square = total_square + square_in[d - 1]
    inverse = lax.rsqrt(total_square / (xs_ref.shape[1] * head_size) + norm_epsilon)
    inverse = jnp.broadcast_to(inverse[0:1, :], (LANES, rows)).T
    inverse = jnp.concatenate([inverse] * (WIDE // LANES), axis=1)
    for c in range(chunks):
        lanes = slice(c * WIDE, (c + 1) * WIDE)
        out_ref[:, lanes] = (gated[c] * inverse * gain_ref[:, lanes]).astype(bf16)

    def drain(c, _):
        for part in range(SUBS):
            pair_copy(c, part).wait_send()

            @pl.when(has_chain_out)
            def _():
                chain_copy(c, part).wait_send()

        return 0

    lax.fori_loop(0, chunks, drain, 0)
    d_copy().wait_send()
    for d in range(1, head_size):
        square_copy(d).wait_send()

    @pl.when(has_next)
    def _():
        for copy in halo_copies():
            copy.wait_send()


def solution(mesh):
    seq_size = mesh.shape["seq"]
    head_size = mesh.shape["head"]

    def per_device(
        xs, gate_z, b_in, c_in, dt, log_decay, d_skip, conv_x, conv_b, conv_c, gain, doc_lengths
    ):
        rows, width = xs.shape
        heads = dt.shape[1]
        groups = b_in.shape[1] // STATE
        chunks = width // WIDE
        blocks = rows // BLOCK
        per_chunk = WIDE // HEAD_DIM
        vmem = pltpu.VMEM
        dma = pltpu.SemaphoreType.DMA
        state = vmem((chunks, STATE, WIDE), bf16)
        return pl.pallas_call(
            functools.partial(kernel, seq_size, head_size),
            out_shape=pltpu.VMEM((rows, width), bf16),
            in_specs=[pl.BlockSpec(memory_space=pltpu.SMEM)]
            + [pl.BlockSpec(memory_space=pltpu.HBM)] * 2
            + [pl.BlockSpec(memory_space=pltpu.VMEM)] * 9,
            out_specs=pl.BlockSpec(memory_space=pltpu.VMEM),
            scratch_shapes=[
                vmem((rows, width), bf16),
                vmem((rows, width), bf16),
                vmem((HALO, width), bf16),
                vmem((HALO, groups * STATE), bf16),
                vmem((HALO, groups * STATE), bf16),
                state,
                state,
                state,
                state,
                state,
                vmem((16, LANES), bf16),
                vmem((16, LANES), bf16),
                vmem((3, rows, LANES), f32),
                vmem((chunks, rows, WIDE), bf16),
                vmem((chunks, rows, WIDE), bf16),
                vmem((groups, rows, STATE), bf16),
                vmem((groups, rows, STATE), bf16),
                vmem((groups, blocks, STATE, BLOCK), bf16),
                vmem((groups, blocks, BLOCK, BLOCK), f32),
                vmem((blocks, chunks, 8, BLOCK), f32),
                vmem((6, rows, LANES), bf16),
                vmem((chunks, rows, WIDE), f32),
                vmem((rows, LANES), f32),
                vmem((8, rows), f32),
                vmem((head_size - 1, 8, rows), f32),
                dma((3,)),
                dma((3,)),
                dma,
                dma,
                dma((chunks, SUBS)),
                dma((chunks, SUBS)),
                dma((chunks, SUBS)),
                dma((chunks, SUBS)),
                dma((head_size - 1,)),
                dma((head_size - 1,)),
                dma((2,)),
            ],
            compiler_params=pltpu.CompilerParams(
                collective_id=0, has_side_effects=True, vmem_limit_bytes=60_000_000
            ),
        )(
            doc_lengths,
            xs,
            gate_z,
            b_in,
            c_in,
            dt.T,
            log_decay.T,
            d_skip.reshape(1, -1),
            conv_x,
            conv_b,
            conv_c,
            gain.reshape(1, -1),
        )

    whole = P("seq", "head")
    across = P(None, "head")
    return jax.shard_map(
        per_device,
        mesh=mesh,
        in_specs=(
            whole,
            whole,
            whole,
            whole,
            whole,
            whole,
            P("head"),
            across,
            across,
            across,
            P("head"),
            P(),
        ),
        out_specs=whole,
        check_vma=False,
    )
```

profile of v0, /device:TPU:25, one launch (start us, length us, event | category | flops | bytes accessed | tf_op | source)
XLA Modules:
  0.0 34.3 jit_solution(14962116420054277052)
XLA Ops:
  0.0 33.3 %shard_map.118 = bf16[256,2048]{1,0:T(8,128)(2,1)S(1)} custom-call(s32[4]{0:T(128)} %lengths_ref.1, bf16[256,2048]{1,0:T(8,128)(2,1)} %xs_hbm.1, bf16[256,2048]{1,0:T(8,128)(2,1)} %z_hbm.1, bf16[256,256]{1,0:T(8,128)(2,1)} %b_ref.1, bf16[256,256]{1,0:T(8,128)(2,1)} %c_ref.1, f32[32,256]{1,0:T(8,128)} %bitcast.4, f32[32,256]{1,0:T(8,128)} %bitcast.5, ...), custom_call_target="tpu_custom_call" | custom-call | tf_op jit(solution)/shard_map/pallas_call | solution.py:481
  33.3 1.0 %copy.14 = bf16[256,2048]{1,0:T(8,128)(2,1)} copy(bf16[256,2048]{1,0:T(8,128)(2,1)S(1)} %shard_map.118) | data formatting | bytes 2097152
where the time goes:
time: 34.4 us; the launch traced here: 34.3 us
  Pallas kernels  33.3 us (97%)
  local copies, waits for them, and re-layouts  0.97 us (3%)
    pallas_call x1, Pallas kernels, per_device(): pl.pallas_call(functools.partial(kernel, seq_size, head_size), out_shape=...  33.3 us
    unnamed x1, local copies, waits for them, and re-layouts  0.97 us

commit v1 on v0

--- a/solution.py
+++ b/solution.py
@@ -13,7 +13,7 @@
 LANES = 128
 WIDE = 256
 HALO = 16
-SUBS = 2
+SUBS = 4
 norm_epsilon = 1e-05
 
 MESH = pl.DeviceIdType.MESH
@@ -63,10 +63,13 @@
     halo_b,
     halo_c,
     own_s,
-    pair_s,
+    first_s,
+    enter,
+    near_in,
     chain_out,
     chain_in,
-    first_s,
+    back_out,
+    back_in,
     d_own,
     d_pair,
     masks,
@@ -78,6 +81,7 @@
     score,
     cum_turned,
     packed,
+    hot,
     gated,
     square,
     square_own,
@@ -86,10 +90,12 @@
     halo_recv,
     d_send,
     d_recv,
-    pair_send,
-    pair_recv,
+    near_send,
+    near_recv,
     chain_send,
     chain_recv,
+    back_send,
+    back_recv,
     square_send,
     square_recv,
     load_sem,
@@ -101,14 +107,29 @@
     per_chunk = WIDE // HEAD_DIM
     blocks = rows // BLOCK
     docs = lengths_ref.shape[0]
+    n = chunks // 4
+    events = 3 * n
     k = lax.axis_index("seq")
     me = lax.axis_index("head")
     r = lax.rem(k, 2)
+    hop = k // 2
     partner = k + 1 - 2 * r
+    keep = 2 * n + r * n
+    give = 3 * n - r * n
+    even = r == 0
     has_prev = k > 0
     has_next = k + 1 < seq_size
     has_chain_in = k > 1
     has_chain_out = k + 2 < seq_size
+
+    def work_chunk(p):
+        c = jnp.where(p < 3 * n, p - n, keep + p - 3 * n)
+        c = jnp.where(p < 2 * n, p - n, c)
+        return jnp.where(p < n, give + p, c)
+
+    def event_chunk(e):
+        c = jnp.where(e < 2 * n, keep + e - n, e - n)
+        return jnp.where(e < n, e, c)
 
     def halo_copies():
         pairs = ((xs_hbm, halo_x), (b_ref, halo_b), (c_ref, halo_c))
@@ -134,25 +155,37 @@
             device_id_type=MESH,
         )
 
-    def pair_copy(c, part):
-        lines = pl.ds(part * (STATE // SUBS), STATE // SUBS)
+    def lines_of(part):
+        return pl.ds(part * (STATE // SUBS), STATE // SUBS)
+
+    def near_copy(i, part):
+        source = jnp.where(i < n, give + i, i)
         return pltpu.make_async_remote_copy(
-            src_ref=own_s.at[c, lines],
-            dst_ref=pair_s.at[c, lines],
-            send_sem=pair_send.at[c, part],
-            recv_sem=pair_recv.at[c, part],
+            src_ref=own_s.at[source, lines_of(part)],
+            dst_ref=near_in.at[i, lines_of(part)],
+            send_sem=near_send.at[i, part],
+            recv_sem=near_recv.at[i, part],
             device_id={"seq": partner},
             device_id_type=MESH,
         )
 
-    def chain_copy(c, part):
-        lines = pl.ds(part * (STATE // SUBS), STATE // SUBS)
+    def chain_copy(e, part):
         return pltpu.make_async_remote_copy(
-            src_ref=chain_out.at[c, lines],
-            dst_ref=chain_in.at[c, lines],
-            send_sem=chain_send.at[c, part],
-            recv_sem=chain_recv.at[c, part],
+            src_ref=chain_out.at[e, lines_of(part)],
+            dst_ref=chain_in.at[e, lines_of(part)],
+            send_sem=chain_send.at[e, part],
+            recv_sem=chain_recv.at[e, part],
             device_id={"seq": k + 2},
+            device_id_type=MESH,
+        )
+
+    def back_copy(e, part):
+        return pltpu.make_async_remote_copy(
+            src_ref=back_out.at[e, lines_of(part)],
+            dst_ref=back_in.at[e, lines_of(part)],
+            send_sem=back_send.at[e, part],
+            recv_sem=back_recv.at[e, part],
+            device_id={"seq": partner},
             device_id_type=MESH,
         )
 
@@ -189,6 +222,7 @@
     expected = head_size - 1
     for there in (has_prev, has_next, has_chain_in, has_chain_out):
         expected = expected + there.astype(jnp.int32)
+
     @pl.when(k == 0)
     def _():
         halo_x[...] = jnp.zeros_like(halo_x)
@@ -199,25 +233,29 @@
     def _():
         chain_in[...] = jnp.zeros_like(chain_in)
 
+    near_in[2 * n] = jnp.zeros_like(near_in[2 * n])
+    back_in[2 * n] = jnp.zeros_like(back_in[2 * n])
+    for i in range(n):
+        enter[give + i] = jnp.zeros_like(enter[give + i])
+
     starts = []
     running = jnp.int32(0)
     for j in range(docs):
         starts.append(running)
         running = running + lengths_ref[j]
 
-    def doc_at(position):
+    def start_at(position):
         found = jnp.full_like(position, -1)
         for start in starts:
-            found = found + jnp.where(start <= position, 1, 0)
+            found = jnp.where(start <= position, start, found)
         return found
 
     base = k * rows
     column = base + lax.broadcasted_iota(jnp.int32, (rows, LANES), 0)
-    doc_column = doc_at(column)
+    own_start = start_at(column)
     for d in range(1, 4):
-        masks[d - 1] = jnp.where(doc_at(column - d) == doc_column, 1.0, 0.0).astype(f32)
-    entries = [doc_at(base + b * BLOCK - 1) for b in range(blocks)]
-    lasts = [doc_at(base + (b + 1) * BLOCK - 1) for b in range(blocks)]
+        masks[d - 1] = jnp.where(column - own_start >= d, 1.0, 0.0).astype(f32)
+    lasts = [start_at(base + (b + 1) * BLOCK - 1) for b in range(blocks)]
 
     pl.semaphore_wait(barrier, expected)
 
@@ -242,9 +280,9 @@
         here = slice(b * BLOCK, (b + 1) * BLOCK)
         parts = dot(lower, split(decay_rows[here, :]))
         cum = parts[:, :heads] + parts[:, heads : 2 * heads] + parts[:, 2 * heads : 3 * heads]
-        doc = doc_column[here, :heads]
-        ends.append(jnp.where(doc == lasts[b], jnp.exp(cum[BLOCK - 1 :, :] - cum), 0.0))
-        enters.append(jnp.where(doc == entries[b], jnp.exp(cum), 0.0))
+        begun = own_start[here, :heads]
+        ends.append(jnp.where(begun == lasts[b], jnp.exp(cum[BLOCK - 1 :, :] - cum), 0.0))
+        enters.append(jnp.where(begun < base + b * BLOCK, jnp.exp(cum), 0.0))
         cums.append(cum)
         wide = jnp.concatenate([cum, jnp.zeros((BLOCK, LANES - heads), f32)], axis=1)
         turned = wide.T
@@ -252,13 +290,13 @@
             cum_turned[b, c, 0:per_chunk, :] = turned[c * per_chunk : (c + 1) * per_chunk, :]
     carry0 = enters[0][BLOCK - 1 :, :]
     carry1 = enters[1][BLOCK - 1 :, :]
+    d_own[...] = split(jnp.broadcast_to(carry0 * carry1, (16, heads)))
+    d_copy().start()
     packed[0] = split(dt_rows)
     packed[1] = split(jnp.concatenate(ends, axis=0))
     packed[2] = split(jnp.concatenate([enters[0], enters[1] * carry0], axis=0))
     packed[3] = split(jnp.concatenate([enters[0], enters[1]], axis=0))
     packed[4] = split(jnp.concatenate(cums, axis=0))
-    d_own[...] = split(jnp.broadcast_to(carry0 * carry1, (16, heads)))
-    d_copy().start()
     few = split(
         jnp.concatenate(
             [jnp.broadcast_to(carry1, (8, heads)), jnp.broadcast_to(skip_ref[...], (8, heads))], 0
@@ -291,7 +329,6 @@
     for g in range(groups):
         lanes = slice(g * STATE, (g + 1) * STATE)
         b_conv[g] = convolve(b_ref[:, lanes], conv_b_ref[:, lanes])
-        c_conv[g] = convolve(c_ref[:, lanes], conv_c_ref[:, lanes])
         b_turned[g, 1] = b_conv[g, BLOCK:, :].astype(f32).T.astype(bf16)
 
     load_x.wait()
@@ -299,7 +336,8 @@
     def lanes_of(c, half):
         return pl.ds(pl.multiple_of(c * WIDE + half * LANES, LANES), LANES)
 
-    def conv_step(c, _):
+    def conv_step(p, _):
+        c = work_chunk(p)
         for half in range(WIDE // LANES):
             lanes = lanes_of(c, half)
             x_conv[c, :, half * LANES : (half + 1) * LANES] = convolve(
@@ -317,10 +355,10 @@
     for g in range(groups):
         lanes = slice(g * STATE, (g + 1) * STATE)
         b_conv[g, 0:HALO, :] = convolve_top(b_ref[0:HALO, lanes], halo_b[:, lanes], conv_b_ref[:, lanes])
-        c_conv[g, 0:HALO, :] = convolve_top(c_ref[0:HALO, lanes], halo_c[:, lanes], conv_c_ref[:, lanes])
         b_turned[g, 0] = b_conv[g, :BLOCK, :].astype(f32).T.astype(bf16)
 
-    def state_step(c, _):
+    def state_step(p, _):
+        c = work_chunk(p)
         g = c // (chunks // groups)
         for half in range(WIDE // LANES):
             lanes = lanes_of(c, half)
@@ -329,6 +367,7 @@
             )
         x = x_conv[c]
         one_hot = spread(c, HEAD_DIM)
+        hot[c] = one_hot
         product = (dot(packed[0], one_hot) * x.astype(f32)).astype(bf16)
         scaled[c] = product
         weighted = (dot(packed[1], one_hot) * product.astype(f32)).astype(bf16)
@@ -336,17 +375,43 @@
         state1 = dot(b_turned[g, 1], weighted[BLOCK:])
         few = dot(packed[5, 0:16, :], one_hot)
         first_s[c] = state0.astype(bf16)
-        own_s[c] = (few[0:1, :] * state0 + state1).astype(bf16)
-        for part in range(SUBS):
-            pair_copy(c, part).start()
+        state = (few[0:1, :] * state0 + state1).astype(bf16)
+        own_s[c] = state
+
+        @pl.when(p < n)
+        def _():
+            for part in range(SUBS):
+                near_copy(p, part).start()
+
+        @pl.when((p >= 2 * n) & (p < 3 * n))
+        def _():
+            for part in range(SUBS):
+                near_copy(p - n, part).start()
+
+        @pl.when(p == n)
+        def _():
+            d_copy().wait_recv()
+
+        @pl.when((p >= n) & (p < 2 * n) & (hop == 0) & has_chain_out)
+        def _():
+            decay_pair = dot(d_pair[...], one_hot)[0:1, :]
+            wide = state.astype(f32)
+            chain_out[p - n] = jnp.where(even, decay_pair * wide, wide).astype(bf16)
+            for part in range(SUBS):
+                chain_copy(p - n, part).start()
+
         return 0
 
     lax.fori_loop(0, chunks, state_step, 0)
+
+    for g in range(groups):
+        lanes = slice(g * STATE, (g + 1) * STATE)
+        c_conv[g] = convolve(c_ref[:, lanes], conv_c_ref[:, lanes])
+        c_conv[g, 0:HALO, :] = convolve_top(c_ref[0:HALO, lanes], halo_c[:, lanes], conv_c_ref[:, lanes])
 
     for b in range(blocks):
         here = slice(b * BLOCK, (b + 1) * BLOCK)
-        doc_row = doc_at(base + b * BLOCK + lax.broadcasted_iota(jnp.int32, (8, BLOCK), 1))[0:1, :]
-        allowed = (doc_column[here, :] == doc_row) & (s_index <= t_index)
+        allowed = (base + b * BLOCK + s_index >= own_start[here, :]) & (s_index <= t_index)
         for g in range(groups):
             value = lax.dot_general(
                 c_conv[g, here, :],
@@ -357,39 +422,11 @@
             score[g, b] = jnp.where(allowed, value, 0.0)
 
     square[...] = jnp.zeros_like(square)
-    d_copy().wait_recv()
     load_z.wait()
-    even = r == 0
-
-    def main_step(c, _):
+
+    def local_step(c, _):
         g = c // (chunks // groups)
-        one_hot = spread(c, HEAD_DIM)
-        decay_own = dot(d_own[...], one_hot)[0:1, :]
-        decay_pair = dot(d_pair[...], one_hot)[0:1, :]
-        decay_first = jnp.where(even, decay_own, decay_pair)
-        decay_second = jnp.where(even, decay_pair, decay_own)
-        pieces = []
-        for part in range(SUBS):
-            lines = pl.ds(part * (STATE // SUBS), STATE // SUBS)
-            pair_copy(c, part).wait_recv()
-
-            @pl.when(has_chain_in)
-            def _():
-                chain_copy(c, part).wait_recv()
-
-            own = own_s[c, lines].astype(f32)
-            other = pair_s[c, lines].astype(f32)
-            before = chain_in[c, lines].astype(f32)
-            middle = jnp.where(even, own, other) + decay_first * before
-            after = jnp.where(even, other, own) + decay_second * middle
-
-            @pl.when(has_chain_out)
-            def _():
-                chain_out[c, lines] = after.astype(bf16)
-                chain_copy(c, part).start()
-
-            pieces.append(jnp.where(even, before, middle).astype(bf16))
-        entering = jnp.concatenate(pieces, axis=0)
+        one_hot = hot[c]
         one_hot_wide = spread(c, BLOCK)
         lane = lax.broadcasted_iota(jnp.int32, (BLOCK, LANES), 1)
         locals_ = []
@@ -414,8 +451,71 @@
         inner = dot(packed[3, BLOCK:, :], one_hot) * dot(c_conv[g, BLOCK:, :], first_s[c])
         few = dot(packed[5, 0:16, :], one_hot)
         total = jnp.concatenate([locals_[0], locals_[1] + inner], axis=0)
-        total = total + few[8:9, :] * x_conv[c].astype(f32)
-        total = total + dot(packed[2], one_hot) * dot(c_conv[g], entering)
+        gated[c] = total + few[8:9, :] * x_conv[c].astype(f32)
+        return 0
+
+    def chain_event(e):
+        c = event_chunk(e)
+        one_hot = hot[c]
+        decay_own = dot(d_own[...], one_hot)[0:1, :]
+        decay_pair = dot(d_pair[...], one_hot)[0:1, :]
+        decay_first = jnp.where(even, decay_own, decay_pair)
+        decay_second = jnp.where(even, decay_pair, decay_own)
+        near = jnp.where(e < n, 2 * n, e - n)
+        for part in range(SUBS):
+            lines = lines_of(part)
+
+            @pl.when(e >= n)
+            def _():
+                near_copy(e - n, part).wait_recv()
+
+            @pl.when(has_chain_in)
+            def _():
+                chain_copy(e, part).wait_recv()
+
+            own = own_s[c, lines].astype(f32)
+            other = near_in[near, lines].astype(f32)
+            before = chain_in[e, lines].astype(f32)
+            middle = jnp.where(even, own, other) + decay_first * before
+            after = jnp.where(even, other, own) + decay_second * middle
+
+            @pl.when(has_chain_out & ((e >= n) | has_chain_in))
+            def _():
+                chain_out[e, lines] = after.astype(bf16)
+                chain_copy(e, part).start()
+
+            @pl.when(e < 2 * n)
+            def _():
+                back_out[e, lines] = jnp.where(even, middle, before).astype(bf16)
+
+                @pl.when(has_chain_in)
+                def _():
+                    back_copy(e, part).start()
+
+            enter[c, lines] = jnp.where(even, before, middle).astype(bf16)
+
+        @pl.when((e == 2 * n - 1) & (hop == 0))
+        def _():
+            for other_e in range(2 * n):
+                for part in range(SUBS):
+                    back_copy(other_e, part).start()
+
+    def last_step(f, _):
+        t = f - 2 * n
+        late = jnp.where(lax.rem(t, 2) == 0, n + t // 2, give + t // 2)
+        c = jnp.where(f < n, keep + f, jnp.where(f < 2 * n, f - n, late))
+        added = (f >= n) & ((f < 2 * n) | (lax.rem(f, 2) == 1))
+        slot = jnp.where(f < 2 * n, f - n, n + t // 2)
+        slot = jnp.where(added, slot, 2 * n)
+        g = c // (chunks // groups)
+
+        @pl.when(added)
+        def _():
+            for part in range(SUBS):
+                back_copy(slot, part).wait_recv()
+
+        entering = (enter[c].astype(f32) + back_in[slot].astype(f32)).astype(bf16)
+        total = gated[c] + dot(packed[2], hot[c]) * dot(c_conv[g], entering)
         lanes = pl.ds(pl.multiple_of(c * WIDE, WIDE), WIDE)
         value = total * silu(z_ref[:, lanes].astype(f32))
         gated[c] = value
@@ -423,12 +523,54 @@
         square[...] += power[:, :LANES] + power[:, LANES:]
         return 0
 
-    lax.fori_loop(0, chunks, main_step, 0)
+    def locals_before(e):
+        count = jnp.where(hop == 0, 2 * e - 3 * n // 2, chunks)
+        count = jnp.where(hop == 1, 2 * e + n, count)
+        count = jnp.where(e >= events - 1, chunks, count)
+        return jnp.clip(jnp.where(e < 0, 0, count), 0, chunks)
+
+    def lasts_after(e):
+        count = jnp.where(e < 2 * n - 1, 0, 2 * (e + 1) - 2 * n)
+        count = jnp.where((hop == 0) | (locals_before(e) < chunks), 0, count)
+        return jnp.where(e >= events - 1, chunks, count)
+
+    def outer(e, _):
+        lax.fori_loop(locals_before(e - 1), locals_before(e), local_step, 0)
+        chain_event(e)
+        lax.fori_loop(lasts_after(e - 1), lasts_after(e), last_step, 0)
+        return 0
+
+    lax.fori_loop(0, events, outer, 0)
 
     own_square = jnp.sum(square[...].T, axis=0, keepdims=True)
     square_own[...] = jnp.broadcast_to(own_square, square_own.shape)
     for d in range(1, head_size):
         square_copy(d).start()
+
+    def drain_near(i, _):
+        for part in range(SUBS):
+            near_copy(i, part).wait_send()
+            back_copy(i, part).wait_send()
+        return 0
+
+    def drain_chain(e, _):
+        for part in range(SUBS):
+            chain_copy(e, part).wait_send()
+        return 0
+
+    lax.fori_loop(0, 2 * n, drain_near, 0)
+
+    @pl.when(has_chain_out)
+    def _():
+        lax.fori_loop(0, events, drain_chain, 0)
+
+    d_copy().wait_send()
+
+    @pl.when(has_next)
+    def _():
+        for copy in halo_copies():
+            copy.wait_send()
+
     for d in range(1, head_size):
         square_copy(d).wait_recv()
     total_square = square_own[...]
@@ -440,26 +582,8 @@
     for c in range(chunks):
         lanes = slice(c * WIDE, (c + 1) * WIDE)
         out_ref[:, lanes] = (gated[c] * inverse * gain_ref[:, lanes]).astype(bf16)
-
-    def drain(c, _):
-        for part in range(SUBS):
-            pair_copy(c, part).wait_send()
-
-            @pl.when(has_chain_out)
-            def _():
-                chain_copy(c, part).wait_send()
-
-        return 0
-
-    lax.fori_loop(0, chunks, drain, 0)
-    d_copy().wait_send()
     for d in range(1, head_size):
         square_copy(d).wait_send()
-
-    @pl.when(has_next)
-    def _():
-        for copy in halo_copies():
-            copy.wait_send()
 
 
 def solution(mesh):
@@ -477,7 +601,11 @@
         per_chunk = WIDE // HEAD_DIM
         vmem = pltpu.VMEM
         dma = pltpu.SemaphoreType.DMA
-        state = vmem((chunks, STATE, WIDE), bf16)
+        n = chunks // 4
+
+        def states(count):
+            return vmem((count, STATE, WIDE), bf16)
+
         return pl.pallas_call(
             functools.partial(kernel, seq_size, head_size),
             out_shape=pltpu.VMEM((rows, width), bf16),
@@ -491,11 +619,14 @@
                 vmem((HALO, width), bf16),
                 vmem((HALO, groups * STATE), bf16),
                 vmem((HALO, groups * STATE), bf16),
-                state,
-                state,
-                state,
-                state,
-                state,
+                states(chunks),
+                states(chunks),
+                states(chunks),
+                states(2 * n + 1),
+                states(3 * n),
+                states(3 * n),
+                states(2 * n),
+                states(2 * n + 1),
                 vmem((16, LANES), bf16),
                 vmem((16, LANES), bf16),
                 vmem((3, rows, LANES), f32),
@@ -507,6 +638,7 @@
                 vmem((groups, blocks, BLOCK, BLOCK), f32),
                 vmem((blocks, chunks, 8, BLOCK), f32),
                 vmem((6, rows, LANES), bf16),
+                vmem((chunks, LANES, WIDE), bf16),
                 vmem((chunks, rows, WIDE), f32),
                 vmem((rows, LANES), f32),
                 vmem((8, rows), f32),
@@ -515,10 +647,12 @@
                 dma((3,)),
                 dma,
                 dma,
-                dma((chunks, SUBS)),
-                dma((chunks, SUBS)),
-                dma((chunks, SUBS)),
-                dma((chunks, SUBS)),
+                dma((2 * n, SUBS)),
+                dma((2 * n, SUBS)),
+                dma((3 * n, SUBS)),
+                dma((3 * n, SUBS)),
+                dma((2 * n, SUBS)),
+                dma((2 * n, SUBS)),
                 dma((head_size - 1,)),
                 dma((head_size - 1,)),
                 dma((2,)),

time: 34.4 us -> 32.1 us (0.933)
  Pallas kernels: 33.3 us -> 31 us
    pallas_call x1, Pallas kernels: 33.3 us -> 31 us  [per_device(): pl.pallas_call(functools.partial(kernel, seq_size, head_size), out_shape=...]
where the time goes in v1:
time: 32.1 us; the launch traced here: 32 us
  Pallas kernels  31 us (97%)
  local copies, waits for them, and re-layouts  0.97 us (3%)
    pallas_call x1, Pallas kernels, per_device(): pl.pallas_call(functools.partial(kernel, seq_size, head_size), out_shape=...  31 us
    unnamed x1, local copies, waits for them, and re-layouts  0.97 us

profile of v1, /device:TPU:25, one launch (start us, length us, event | category | flops | bytes accessed | tf_op | source)
XLA Modules:
  0.0 32.0 jit_solution(1268711455685451974)
XLA Ops:
  0.0 31.0 %shard_map.118 = bf16[256,2048]{1,0:T(8,128)(2,1)S(1)} custom-call(s32[4]{0:T(128)} %lengths_ref.1, bf16[256,2048]{1,0:T(8,128)(2,1)} %xs_hbm.1, bf16[256,2048]{1,0:T(8,128)(2,1)} %z_hbm.1, bf16[256,256]{1,0:T(8,128)(2,1)} %b_ref.1, bf16[256,256]{1,0:T(8,128)(2,1)} %c_ref.1, f32[32,256]{1,0:T(8,128)} %bitcast.4, f32[32,256]{1,0:T(8,128)} %bitcast.5, ...), custom_call_target="tpu_custom_call" | custom-call | tf_op jit(solution)/shard_map/pallas_call | solution.py:609
  31.0 1.0 %copy.14 = bf16[256,2048]{1,0:T(8,128)(2,1)} copy(bf16[256,2048]{1,0:T(8,128)(2,1)S(1)} %shard_map.118) | data formatting | bytes 2097152

commit v2 on v1

--- a/solution.py
+++ b/solution.py
@@ -44,9 +44,22 @@
 def kernel(
     seq_size,
     head_size,
-    lengths_ref,
+    lengths_hbm,
     xs_hbm,
     z_hbm,
+    b_hbm,
+    c_hbm,
+    dt_hbm,
+    decay_hbm,
+    skip_hbm,
+    conv_x_hbm,
+    conv_b_hbm,
+    conv_c_hbm,
+    gain_hbm,
+    out_ref,
+    lengths_ref,
+    xs_ref,
+    z_ref,
     b_ref,
     c_ref,
     dt_ref,
@@ -56,9 +69,9 @@
     conv_b_ref,
     conv_c_ref,
     gain_ref,
-    out_ref,
-    xs_ref,
-    z_ref,
+    tail_x,
+    halo_out,
+    halo_in,
     halo_x,
     halo_b,
     halo_c,
@@ -131,19 +144,15 @@
         c = jnp.where(e < 2 * n, keep + e - n, e - n)
         return jnp.where(e < n, e, c)
 
-    def halo_copies():
-        pairs = ((xs_hbm, halo_x), (b_ref, halo_b), (c_ref, halo_c))
-        return [
-            pltpu.make_async_remote_copy(
-                src_ref=source.at[pl.ds(rows - HALO, HALO)],
-                dst_ref=target,
-                send_sem=halo_send.at[i],
-                recv_sem=halo_recv.at[i],
-                device_id={"seq": k + 1},
-                device_id_type=MESH,
-            )
-            for i, (source, target) in enumerate(pairs)
-        ]
+    def halo_copy():
+        return pltpu.make_async_remote_copy(
+            src_ref=halo_out,
+            dst_ref=halo_in,
+            send_sem=halo_send,
+            recv_sem=halo_recv,
+            device_id={"seq": k + 1},
+            device_id_type=MESH,
+        )
 
     def d_copy():
         return pltpu.make_async_remote_copy(
@@ -199,10 +208,6 @@
             device_id_type=MESH,
         )
 
-    load_x = pltpu.make_async_copy(xs_hbm, xs_ref, load_sem.at[0])
-    load_z = pltpu.make_async_copy(z_hbm, z_ref, load_sem.at[1])
-    load_x.start()
-
     barrier = pltpu.get_barrier_semaphore()
     for step, there in ((-1, has_prev), (1, has_next), (-2, has_chain_in), (2, has_chain_out)):
 
@@ -223,21 +228,50 @@
     for there in (has_prev, has_next, has_chain_in, has_chain_out):
         expected = expected + there.astype(jnp.int32)
 
-    @pl.when(k == 0)
-    def _():
-        halo_x[...] = jnp.zeros_like(halo_x)
-        halo_b[...] = jnp.zeros_like(halo_b)
-        halo_c[...] = jnp.zeros_like(halo_c)
-
-    @pl.when(k < 2)
-    def _():
-        chain_in[...] = jnp.zeros_like(chain_in)
-
-    near_in[2 * n] = jnp.zeros_like(near_in[2 * n])
-    back_in[2 * n] = jnp.zeros_like(back_in[2 * n])
-    for i in range(n):
-        enter[give + i] = jnp.zeros_like(enter[give + i])
-
+    moves = (
+        (xs_hbm.at[pl.ds(rows - HALO, HALO)], tail_x),
+        (lengths_hbm, lengths_ref),
+        (b_hbm, b_ref),
+        (c_hbm, c_ref),
+        (decay_hbm, decay_ref),
+        (dt_hbm, dt_ref),
+        (xs_hbm, xs_ref),
+        (conv_b_hbm, conv_b_ref),
+        (conv_x_hbm, conv_x_ref),
+        (conv_c_hbm, conv_c_ref),
+        (skip_hbm, skip_ref),
+        (gain_hbm, gain_ref),
+        (z_hbm, z_ref),
+    )
+    loads = [
+        pltpu.make_async_copy(source, target, load_sem.at[i])
+        for i, (source, target) in enumerate(moves)
+    ]
+    for load in loads:
+        load.start()
+    (
+        load_tail, load_lengths, load_b, load_c, load_decay, load_dt, load_x,
+        load_conv_b, load_conv_x, load_conv_c, load_skip, load_gain, load_z,
+    ) = loads
+
+    quarter = xs_ref.shape[1] // 4
+    b_width = b_ref.shape[1]
+    halo_row = lax.broadcasted_iota(jnp.int32, (HALO, quarter), 0) // 3
+
+    load_tail.wait()
+    parcel = jnp.zeros((HALO, quarter), f32)
+    for q in range(4):
+        piece = tail_x[:, q * quarter : (q + 1) * quarter].astype(f32)
+        parcel = jnp.where(halo_row == q, pltpu.roll(piece, 3 * q + 3, 0), parcel)
+    load_b.wait()
+    load_c.wait()
+    pieces = [b_ref[rows - HALO :, :].astype(f32), c_ref[rows - HALO :, :].astype(f32)]
+    if quarter > 2 * b_width:
+        pieces.append(jnp.zeros((HALO, quarter - 2 * b_width), f32))
+    piece = pltpu.roll(jnp.concatenate(pieces, axis=1), 15, 0)
+    halo_out[...] = jnp.where(halo_row == 4, piece, parcel).astype(bf16)
+
+    load_lengths.wait()
     starts = []
     running = jnp.int32(0)
     for j in range(docs):
@@ -256,15 +290,15 @@
     for d in range(1, 4):
         masks[d - 1] = jnp.where(column - own_start >= d, 1.0, 0.0).astype(f32)
     lasts = [start_at(base + (b + 1) * BLOCK - 1) for b in range(blocks)]
+    load_decay.wait()
+    load_dt.wait()
+    load_skip.wait()
 
     pl.semaphore_wait(barrier, expected)
 
     @pl.when(has_next)
     def _():
-        for copy in halo_copies():
-            copy.start()
-
-    load_z.start()
+        halo_copy().start()
 
     def turn(v):
         wide = jnp.concatenate([v, jnp.zeros((LANES - heads, rows), f32)], axis=0)
@@ -326,12 +360,14 @@
             total = total + weight[3 - d : 4 - d, :] * shifted
         return silu(total).astype(bf16)
 
+    load_conv_b.wait()
     for g in range(groups):
         lanes = slice(g * STATE, (g + 1) * STATE)
         b_conv[g] = convolve(b_ref[:, lanes], conv_b_ref[:, lanes])
         b_turned[g, 1] = b_conv[g, BLOCK:, :].astype(f32).T.astype(bf16)
 
     load_x.wait()
+    load_conv_x.wait()
 
     def lanes_of(c, half):
         return pl.ds(pl.multiple_of(c * WIDE + half * LANES, LANES), LANES)
@@ -345,12 +381,33 @@
             )
         return 0
 
-    lax.fori_loop(0, chunks, conv_step, 0)
+    lax.fori_loop(0, 3 * n, conv_step, 0)
+
+    @pl.when(k < 2)
+    def _():
+        chain_in[...] = jnp.zeros_like(chain_in)
+
+    near_in[2 * n] = jnp.zeros_like(near_in[2 * n])
+    back_in[2 * n] = jnp.zeros_like(back_in[2 * n])
+    for i in range(n):
+        enter[give + i] = jnp.zeros_like(enter[give + i])
+
+    @pl.when(k == 0)
+    def _():
+        halo_in[...] = jnp.zeros_like(halo_in)
 
     @pl.when(has_prev)
     def _():
-        for copy in halo_copies():
-            copy.wait_recv()
+        halo_copy().wait_recv()
+
+    arrived = halo_in[...].astype(f32)
+    for q in range(4):
+        halo_x[:, q * quarter : (q + 1) * quarter] = pltpu.roll(
+            arrived, HALO - 3 - 3 * q, 0
+        ).astype(bf16)
+    piece = pltpu.roll(arrived, 1, 0)
+    halo_b[...] = piece[:, :b_width].astype(bf16)
+    halo_c[...] = piece[:, b_width : 2 * b_width].astype(bf16)
 
     for g in range(groups):
         lanes = slice(g * STATE, (g + 1) * STATE)
@@ -402,7 +459,10 @@
 
         return 0
 
-    lax.fori_loop(0, chunks, state_step, 0)
+    lax.fori_loop(0, 3 * n, state_step, 0)
+    lax.fori_loop(3 * n, chunks, conv_step, 0)
+    lax.fori_loop(3 * n, chunks, state_step, 0)
+    load_conv_c.wait()
 
     for g in range(groups):
         lanes = slice(g * STATE, (g + 1) * STATE)
@@ -423,6 +483,7 @@
 
     square[...] = jnp.zeros_like(square)
     load_z.wait()
+    load_gain.wait()
 
     def local_step(c, _):
         g = c // (chunks // groups)
@@ -568,8 +629,7 @@
 
     @pl.when(has_next)
     def _():
-        for copy in halo_copies():
-            copy.wait_send()
+        halo_copy().wait_send()
 
     for d in range(1, head_size):
         square_copy(d).wait_recv()
@@ -609,13 +669,24 @@
         return pl.pallas_call(
             functools.partial(kernel, seq_size, head_size),
             out_shape=pltpu.VMEM((rows, width), bf16),
-            in_specs=[pl.BlockSpec(memory_space=pltpu.SMEM)]
-            + [pl.BlockSpec(memory_space=pltpu.HBM)] * 2
-            + [pl.BlockSpec(memory_space=pltpu.VMEM)] * 9,
+            in_specs=[pl.BlockSpec(memory_space=pltpu.HBM)] * 12,
             out_specs=pl.BlockSpec(memory_space=pltpu.VMEM),
             scratch_shapes=[
+                pltpu.SMEM(doc_lengths.shape, jnp.int32),
                 vmem((rows, width), bf16),
                 vmem((rows, width), bf16),
+                vmem((rows, groups * STATE), bf16),
+                vmem((rows, groups * STATE), bf16),
+                vmem((heads, rows), f32),
+                vmem((heads, rows), f32),
+                vmem((1, heads), f32),
+                vmem((4, width), f32),
+                vmem((4, groups * STATE), f32),
+                vmem((4, groups * STATE), f32),
+                vmem((1, width), f32),
+                vmem((HALO, width), bf16),
+                vmem((HALO, width // 4), bf16),
+                vmem((HALO, width // 4), bf16),
                 vmem((HALO, width), bf16),
                 vmem((HALO, groups * STATE), bf16),
                 vmem((HALO, groups * STATE), bf16),
@@ -643,8 +714,8 @@
                 vmem((rows, LANES), f32),
                 vmem((8, rows), f32),
                 vmem((head_size - 1, 8, rows), f32),
-                dma((3,)),
-                dma((3,)),
+                dma,
+                dma,
                 dma,
                 dma,
                 dma((2 * n, SUBS)),
@@ -655,7 +726,7 @@
                 dma((2 * n, SUBS)),
                 dma((head_size - 1,)),
                 dma((head_size - 1,)),
-                dma((2,)),
+                dma((13,)),
             ],
             compiler_params=pltpu.CompilerParams(
                 collective_id=0, has_side_effects=True, vmem_limit_bytes=60_000_000

time: 32.1 us -> 31.3 us (0.975)
  Pallas kernels: 31 us -> 30.1 us
    pallas_call x1, Pallas kernels: 31 us -> 30.1 us  [per_device(): pl.pallas_call(functools.partial(kernel, seq_size, head_size), out_shape=...]
where the time goes in v2:
time: 31.3 us; the launch traced here: 31.1 us
  Pallas kernels  30.1 us (96%)
  local copies, waits for them, and re-layouts  0.97 us (3%)
    pallas_call x1, Pallas kernels, per_device(): pl.pallas_call(functools.partial(kernel, seq_size, head_size), out_shape=...  30.1 us
    unnamed x1, local copies, waits for them, and re-layouts  0.97 us

profile of v2, /device:TPU:25, one launch (start us, length us, event | category | flops | bytes accessed | tf_op | source)
XLA Modules:
  0.0 31.1 jit_solution(2852092698508612630)
XLA Ops:
  0.0 30.1 %shard_map.118 = bf16[256,2048]{1,0:T(8,128)(2,1)S(1)} custom-call(s32[4]{0:T(128)} %lengths_hbm.1, bf16[256,2048]{1,0:T(8,128)(2,1)} %xs_hbm.1, bf16[256,2048]{1,0:T(8,128)(2,1)} %z_hbm.1, bf16[256,256]{1,0:T(8,128)(2,1)} %b_hbm.1, bf16[256,256]{1,0:T(8,128)(2,1)} %c_hbm.1, f32[32,256]{1,0:T(8,128)} %bitcast.4, f32[32,256]{1,0:T(8,128)} %bitcast.5, ...), custom_call_target="tpu_custom_call" | custom-call | tf_op jit(solution)/shard_map/pallas_call | solution.py:669
  30.1 1.0 %copy.14 = bf16[256,2048]{1,0:T(8,128)(2,1)} copy(bf16[256,2048]{1,0:T(8,128)(2,1)S(1)} %shard_map.118) | data formatting | bytes 2097152

commit v3 on v2

--- a/solution.py
+++ b/solution.py
@@ -95,6 +95,7 @@
     cum_turned,
     packed,
     hot,
+    hot_wide,
     gated,
     square,
     square_own,
@@ -294,12 +295,6 @@
     load_dt.wait()
     load_skip.wait()
 
-    pl.semaphore_wait(barrier, expected)
-
-    @pl.when(has_next)
-    def _():
-        halo_copy().start()
-
     def turn(v):
         wide = jnp.concatenate([v, jnp.zeros((LANES - heads, rows), f32)], axis=0)
         return wide.T[:, :heads]
@@ -318,19 +313,11 @@
         ends.append(jnp.where(begun == lasts[b], jnp.exp(cum[BLOCK - 1 :, :] - cum), 0.0))
         enters.append(jnp.where(begun < base + b * BLOCK, jnp.exp(cum), 0.0))
         cums.append(cum)
-        wide = jnp.concatenate([cum, jnp.zeros((BLOCK, LANES - heads), f32)], axis=1)
-        turned = wide.T
-        for c in range(chunks):
-            cum_turned[b, c, 0:per_chunk, :] = turned[c * per_chunk : (c + 1) * per_chunk, :]
     carry0 = enters[0][BLOCK - 1 :, :]
     carry1 = enters[1][BLOCK - 1 :, :]
     d_own[...] = split(jnp.broadcast_to(carry0 * carry1, (16, heads)))
-    d_copy().start()
     packed[0] = split(dt_rows)
     packed[1] = split(jnp.concatenate(ends, axis=0))
-    packed[2] = split(jnp.concatenate([enters[0], enters[1] * carry0], axis=0))
-    packed[3] = split(jnp.concatenate([enters[0], enters[1]], axis=0))
-    packed[4] = split(jnp.concatenate(cums, axis=0))
     few = split(
         jnp.concatenate(
             [jnp.broadcast_to(carry1, (8, heads)), jnp.broadcast_to(skip_ref[...], (8, heads))], 0
@@ -368,6 +355,13 @@
 
     load_x.wait()
     load_conv_x.wait()
+    pl.semaphore_wait(barrier, expected)
+
+    @pl.when(has_next)
+    def _():
+        halo_copy().start()
+
+    d_copy().start()
 
     def lanes_of(c, half):
         return pl.ds(pl.multiple_of(c * WIDE + half * LANES, LANES), LANES)
@@ -382,6 +376,13 @@
         return 0
 
     lax.fori_loop(0, 3 * n, conv_step, 0)
+
+    def hot_step(c, _):
+        hot[c] = spread(c, HEAD_DIM)
+        hot_wide[c] = spread(c, BLOCK)
+        return 0
+
+    lax.fori_loop(0, chunks, hot_step, 0)
 
     @pl.when(k < 2)
     def _():
@@ -423,8 +424,7 @@
                 xs_ref[0:HALO, lanes], halo_x[:, lanes], conv_x_ref[:, lanes]
             )
         x = x_conv[c]
-        one_hot = spread(c, HEAD_DIM)
-        hot[c] = one_hot
+        one_hot = hot[c]
         product = (dot(packed[0], one_hot) * x.astype(f32)).astype(bf16)
         scaled[c] = product
         weighted = (dot(packed[1], one_hot) * product.astype(f32)).astype(bf16)
@@ -463,6 +463,15 @@
     lax.fori_loop(3 * n, chunks, conv_step, 0)
     lax.fori_loop(3 * n, chunks, state_step, 0)
     load_conv_c.wait()
+
+    packed[2] = split(jnp.concatenate([enters[0], enters[1] * carry0], axis=0))
+    packed[3] = split(jnp.concatenate([enters[0], enters[1]], axis=0))
+    packed[4] = split(jnp.concatenate(cums, axis=0))
+    for b in range(blocks):
+        wide = jnp.concatenate([cums[b], jnp.zeros((BLOCK, LANES - heads), f32)], axis=1)
+        turned = wide.T
+        for c in range(chunks):
+            cum_turned[b, c, 0:per_chunk, :] = turned[c * per_chunk : (c + 1) * per_chunk, :]
 
     for g in range(groups):
         lanes = slice(g * STATE, (g + 1) * STATE)
@@ -488,7 +497,7 @@
     def local_step(c, _):
         g = c // (chunks // groups)
         one_hot = hot[c]
-        one_hot_wide = spread(c, BLOCK)
+        one_hot_wide = hot_wide[c]
         lane = lax.broadcasted_iota(jnp.int32, (BLOCK, LANES), 1)
         locals_ = []
         for b in range(blocks):
@@ -585,23 +594,28 @@
         return 0
 
     def locals_before(e):
-        count = jnp.where(hop == 0, 2 * e - 3 * n // 2, chunks)
-        count = jnp.where(hop == 1, 2 * e + n, count)
-        count = jnp.where(e >= events - 1, chunks, count)
+        count = jnp.where(hop == 0, e - n, chunks)
+        count = jnp.where(hop == 1, e, count)
+        count = jnp.where(hop == 2, e + 3 * n // 2, count)
+        count = jnp.where(e >= events, chunks, count)
         return jnp.clip(jnp.where(e < 0, 0, count), 0, chunks)
 
     def lasts_after(e):
         count = jnp.where(e < 2 * n - 1, 0, 2 * (e + 1) - 2 * n)
-        count = jnp.where((hop == 0) | (locals_before(e) < chunks), 0, count)
-        return jnp.where(e >= events - 1, chunks, count)
+        count = jnp.where(has_chain_out | (locals_before(e) < chunks), 0, count)
+        return jnp.where(e >= events, chunks, count)
 
     def outer(e, _):
         lax.fori_loop(locals_before(e - 1), locals_before(e), local_step, 0)
-        chain_event(e)
+
+        @pl.when(e < events)
+        def _():
+            chain_event(e)
+
         lax.fori_loop(lasts_after(e - 1), lasts_after(e), last_step, 0)
         return 0
 
-    lax.fori_loop(0, events, outer, 0)
+    lax.fori_loop(0, events + 1, outer, 0)
 
     own_square = jnp.sum(square[...].T, axis=0, keepdims=True)
     square_own[...] = jnp.broadcast_to(own_square, square_own.shape)
@@ -710,6 +724,7 @@
                 vmem((blocks, chunks, 8, BLOCK), f32),
                 vmem((6, rows, LANES), bf16),
                 vmem((chunks, LANES, WIDE), bf16),
+                vmem((chunks, LANES, per_chunk * BLOCK), bf16),
                 vmem((chunks, rows, WIDE), f32),
                 vmem((rows, LANES), f32),
                 vmem((8, rows), f32),

time: 31.3 us -> 29 us (0.927)
  Pallas kernels: 30.1 us -> 27.8 us
    pallas_call x1, Pallas kernels: 30.1 us -> 27.8 us  [per_device(): pl.pallas_call(functools.partial(kernel, seq_size, head_size), out_shape=...]
where the time goes in v3:
time: 29 us; the launch traced here: 28.8 us
  Pallas kernels  27.8 us (96%)
  local copies, waits for them, and re-layouts  0.97 us (3%)
    pallas_call x1, Pallas kernels, per_device(): pl.pallas_call(functools.partial(kernel, seq_size, head_size), out_shape=...  27.8 us
    unnamed x1, local copies, waits for them, and re-layouts  0.97 us

profile of v3, /device:TPU:25, one launch (start us, length us, event | category | flops | bytes accessed | tf_op | source)
XLA Modules:
  0.0 28.8 jit_solution(12800165881516098356)
XLA Ops:
  0.0 27.8 %shard_map.118 = bf16[256,2048]{1,0:T(8,128)(2,1)S(1)} custom-call(s32[4]{0:T(128)} %lengths_hbm.1, bf16[256,2048]{1,0:T(8,128)(2,1)} %xs_hbm.1, bf16[256,2048]{1,0:T(8,128)(2,1)} %z_hbm.1, bf16[256,256]{1,0:T(8,128)(2,1)} %b_hbm.1, bf16[256,256]{1,0:T(8,128)(2,1)} %c_hbm.1, f32[32,256]{1,0:T(8,128)} %bitcast.4, f32[32,256]{1,0:T(8,128)} %bitcast.5, ...), custom_call_target="tpu_custom_call" | custom-call | tf_op jit(solution)/shard_map/pallas_call | solution.py:683
  27.9 1.0 %copy.14 = bf16[256,2048]{1,0:T(8,128)(2,1)} copy(bf16[256,2048]{1,0:T(8,128)(2,1)S(1)} %shard_map.118) | data formatting | bytes 2097152

commit v4 on v3

--- a/solution.py
+++ b/solution.py
@@ -14,6 +14,9 @@
 WIDE = 256
 HALO = 16
 SUBS = 4
+NEAR = 2
+CHAIN = 4
+BACK = 2
 norm_epsilon = 1e-05
 
 MESH = pl.DeviceIdType.MESH
@@ -55,8 +58,8 @@
     conv_x_hbm,
     conv_b_hbm,
     conv_c_hbm,
-    gain_hbm,
-    out_ref,
+    gated,
+    inverse_ref,
     lengths_ref,
     xs_ref,
     z_ref,
@@ -68,7 +71,6 @@
     conv_x_ref,
     conv_b_ref,
     conv_c_ref,
-    gain_ref,
     tail_x,
     halo_out,
     halo_in,
@@ -96,7 +98,6 @@
     packed,
     hot,
     hot_wide,
-    gated,
     square,
     square_own,
     square_in,
@@ -138,8 +139,8 @@
 
     def work_chunk(p):
         c = jnp.where(p < 3 * n, p - n, keep + p - 3 * n)
-        c = jnp.where(p < 2 * n, p - n, c)
-        return jnp.where(p < n, give + p, c)
+        c = jnp.where(p < 2 * n, give + p - n, c)
+        return jnp.where(p < n, p, c)
 
     def event_chunk(e):
         c = jnp.where(e < 2 * n, keep + e - n, e - n)
@@ -165,14 +166,14 @@
             device_id_type=MESH,
         )
 
-    def lines_of(part):
-        return pl.ds(part * (STATE // SUBS), STATE // SUBS)
+    def lines_of(part, parts=SUBS):
+        return pl.ds(part * (STATE // parts), STATE // parts)
 
     def near_copy(i, part):
         source = jnp.where(i < n, give + i, i)
         return pltpu.make_async_remote_copy(
-            src_ref=own_s.at[source, lines_of(part)],
-            dst_ref=near_in.at[i, lines_of(part)],
+            src_ref=own_s.at[source, lines_of(part, NEAR)],
+            dst_ref=near_in.at[i, lines_of(part, NEAR)],
             send_sem=near_send.at[i, part],
             recv_sem=near_recv.at[i, part],
             device_id={"seq": partner},
@@ -181,8 +182,8 @@
 
     def chain_copy(e, part):
         return pltpu.make_async_remote_copy(
-            src_ref=chain_out.at[e, lines_of(part)],
-            dst_ref=chain_in.at[e, lines_of(part)],
+            src_ref=chain_out.at[e, lines_of(part, CHAIN)],
+            dst_ref=chain_in.at[e, lines_of(part, CHAIN)],
             send_sem=chain_send.at[e, part],
             recv_sem=chain_recv.at[e, part],
             device_id={"seq": k + 2},
@@ -191,8 +192,8 @@
 
     def back_copy(e, part):
         return pltpu.make_async_remote_copy(
-            src_ref=back_out.at[e, lines_of(part)],
-            dst_ref=back_in.at[e, lines_of(part)],
+            src_ref=back_out.at[e, lines_of(part, BACK)],
+            dst_ref=back_in.at[e, lines_of(part, BACK)],
             send_sem=back_send.at[e, part],
             recv_sem=back_recv.at[e, part],
             device_id={"seq": partner},
@@ -241,7 +242,6 @@
         (conv_x_hbm, conv_x_ref),
         (conv_c_hbm, conv_c_ref),
         (skip_hbm, skip_ref),
-        (gain_hbm, gain_ref),
         (z_hbm, z_ref),
     )
     loads = [
@@ -252,7 +252,7 @@
         load.start()
     (
         load_tail, load_lengths, load_b, load_c, load_decay, load_dt, load_x,
-        load_conv_b, load_conv_x, load_conv_c, load_skip, load_gain, load_z,
+        load_conv_b, load_conv_x, load_conv_c, load_skip, load_z,
     ) = loads
 
     quarter = xs_ref.shape[1] // 4
@@ -435,27 +435,22 @@
         state = (few[0:1, :] * state0 + state1).astype(bf16)
         own_s[c] = state
 
-        @pl.when(p < n)
+        @pl.when((p >= n) & (p < 3 * n))
         def _():
-            for part in range(SUBS):
-                near_copy(p, part).start()
-
-        @pl.when((p >= 2 * n) & (p < 3 * n))
-        def _():
-            for part in range(SUBS):
+            for part in range(NEAR):
                 near_copy(p - n, part).start()
 
-        @pl.when(p == n)
+        @pl.when(p == 0)
         def _():
             d_copy().wait_recv()
 
-        @pl.when((p >= n) & (p < 2 * n) & (hop == 0) & has_chain_out)
+        @pl.when((p < n) & (hop == 0) & has_chain_out)
         def _():
             decay_pair = dot(d_pair[...], one_hot)[0:1, :]
             wide = state.astype(f32)
-            chain_out[p - n] = jnp.where(even, decay_pair * wide, wide).astype(bf16)
-            for part in range(SUBS):
-                chain_copy(p - n, part).start()
+            chain_out[p] = jnp.where(even, decay_pair * wide, wide).astype(bf16)
+            for part in range(CHAIN):
+                chain_copy(p, part).start()
 
         return 0
 
@@ -492,7 +487,6 @@
 
     square[...] = jnp.zeros_like(square)
     load_z.wait()
-    load_gain.wait()
 
     def local_step(c, _):
         g = c // (chunks // groups)
@@ -535,13 +529,17 @@
         for part in range(SUBS):
             lines = lines_of(part)
 
-            @pl.when(e >= n)
-            def _():
-                near_copy(e - n, part).wait_recv()
-
-            @pl.when(has_chain_in)
-            def _():
-                chain_copy(e, part).wait_recv()
+            if part % (SUBS // NEAR) == 0:
+
+                @pl.when(e >= n)
+                def _():
+                    near_copy(e - n, part * NEAR // SUBS).wait_recv()
+
+            if part % (SUBS // CHAIN) == 0:
+
+                @pl.when(has_chain_in)
+                def _():
+                    chain_copy(e, part * CHAIN // SUBS).wait_recv()
 
             own = own_s[c, lines].astype(f32)
             other = near_in[near, lines].astype(f32)
@@ -552,22 +550,25 @@
             @pl.when(has_chain_out & ((e >= n) | has_chain_in))
             def _():
                 chain_out[e, lines] = after.astype(bf16)
-                chain_copy(e, part).start()
+                if (part + 1) % (SUBS // CHAIN) == 0:
+                    chain_copy(e, part * CHAIN // SUBS).start()
 
             @pl.when(e < 2 * n)
             def _():
                 back_out[e, lines] = jnp.where(even, middle, before).astype(bf16)
 
-                @pl.when(has_chain_in)
-                def _():
-                    back_copy(e, part).start()
+                if (part + 1) % (SUBS // BACK) == 0:
+
+                    @pl.when(has_chain_in)
+                    def _():
+                        back_copy(e, part * BACK // SUBS).start()
 
             enter[c, lines] = jnp.where(even, before, middle).astype(bf16)
 
         @pl.when((e == 2 * n - 1) & (hop == 0))
         def _():
             for other_e in range(2 * n):
-                for part in range(SUBS):
+                for part in range(BACK):
                     back_copy(other_e, part).start()
 
     def last_step(f, _):
@@ -581,7 +582,7 @@
 
         @pl.when(added)
         def _():
-            for part in range(SUBS):
+            for part in range(BACK):
                 back_copy(slot, part).wait_recv()
 
         entering = (enter[c].astype(f32) + back_in[slot].astype(f32)).astype(bf16)
@@ -603,7 +604,7 @@
     def lasts_after(e):
         count = jnp.where(e < 2 * n - 1, 0, 2 * (e + 1) - 2 * n)
         count = jnp.where(has_chain_out | (locals_before(e) < chunks), 0, count)
-        return jnp.where(e >= events, chunks, count)
+        return jnp.where(e >= events, chunks, jnp.minimum(count, chunks))
 
     def outer(e, _):
         lax.fori_loop(locals_before(e - 1), locals_before(e), local_step, 0)
@@ -623,13 +624,14 @@
         square_copy(d).start()
 
     def drain_near(i, _):
-        for part in range(SUBS):
+        for part in range(NEAR):
             near_copy(i, part).wait_send()
+        for part in range(BACK):
             back_copy(i, part).wait_send()
         return 0
 
     def drain_chain(e, _):
-        for part in range(SUBS):
+        for part in range(CHAIN):
             chain_copy(e, part).wait_send()
         return 0
 
@@ -652,12 +654,22 @@
         total_square = total_square + square_in[d - 1]
     inverse = lax.rsqrt(total_square / (xs_ref.shape[1] * head_size) + norm_epsilon)
     inverse = jnp.broadcast_to(inverse[0:1, :], (LANES, rows)).T
-    inverse = jnp.concatenate([inverse] * (WIDE // LANES), axis=1)
+    inverse_ref[...] = inverse
+    for d in range(1, head_size):
+        square_copy(d).wait_send()
+
+
+def scale_kernel(gated, inverse_ref, gain_ref, out_hbm, out_ref, sem):
+    chunks = gated.shape[0]
+    inverse = jnp.concatenate([inverse_ref[...]] * (WIDE // LANES), axis=1)
+    copies = []
     for c in range(chunks):
         lanes = slice(c * WIDE, (c + 1) * WIDE)
-        out_ref[:, lanes] = (gated[c] * inverse * gain_ref[:, lanes]).astype(bf16)
-    for d in range(1, head_size):
-        square_copy(d).wait_send()
+        out_ref[c] = (gated[c] * inverse * gain_ref[:, lanes]).astype(bf16)
+        copies.append(pltpu.make_async_copy(out_ref.at[c], out_hbm.at[:, lanes], sem.at[c]))
+        copies[-1].start()
+    for copy in copies:
+        copy.wait()
 
 
 def solution(mesh):
@@ -680,11 +692,11 @@
         def states(count):
             return vmem((count, STATE, WIDE), bf16)
 
-        return pl.pallas_call(
+        gated, inverse = pl.pallas_call(
             functools.partial(kernel, seq_size, head_size),
-            out_shape=pltpu.VMEM((rows, width), bf16),
-            in_specs=[pl.BlockSpec(memory_space=pltpu.HBM)] * 12,
-            out_specs=pl.BlockSpec(memory_space=pltpu.VMEM),
+            out_shape=(vmem((chunks, rows, WIDE), f32), vmem((rows, LANES), f32)),
+            in_specs=[pl.BlockSpec(memory_space=pltpu.HBM)] * 11,
+            out_specs=(pl.BlockSpec(memory_space=pltpu.VMEM),) * 2,
             scratch_shapes=[
                 pltpu.SMEM(doc_lengths.shape, jnp.int32),
                 vmem((rows, width), bf16),
@@ -697,7 +709,6 @@
                 vmem((4, width), f32),
                 vmem((4, groups * STATE), f32),
                 vmem((4, groups * STATE), f32),
-                vmem((1, width), f32),
                 vmem((HALO, width), bf16),
                 vmem((HALO, width // 4), bf16),
                 vmem((HALO, width // 4), bf16),
@@ -725,7 +736,6 @@
                 vmem((6, rows, LANES), bf16),
                 vmem((chunks, LANES, WIDE), bf16),
                 vmem((chunks, LANES, per_chunk * BLOCK), bf16),
-                vmem((chunks, rows, WIDE), f32),
                 vmem((rows, LANES), f32),
                 vmem((8, rows), f32),
                 vmem((head_size - 1, 8, rows), f32),
@@ -733,15 +743,15 @@
                 dma,
                 dma,
                 dma,
-                dma((2 * n, SUBS)),
-                dma((2 * n, SUBS)),
-                dma((3 * n, SUBS)),
-                dma((3 * n, SUBS)),
-                dma((2 * n, SUBS)),
-                dma((2 * n, SUBS)),
+                dma((2 * n, NEAR)),
+                dma((2 * n, NEAR)),
+                dma((3 * n, CHAIN)),
+                dma((3 * n, CHAIN)),
+                dma((2 * n, BACK)),
+                dma((2 * n, BACK)),
                 dma((head_size - 1,)),
                 dma((head_size - 1,)),
-                dma((13,)),
+                dma((12,)),
             ],
             compiler_params=pltpu.CompilerParams(
                 collective_id=0, has_side_effects=True, vmem_limit_bytes=60_000_000
@@ -758,8 +768,15 @@
             conv_x,
             conv_b,
             conv_c,
-            gain.reshape(1, -1),
         )
+        return pl.pallas_call(
+            scale_kernel,
+            out_shape=jax.ShapeDtypeStruct((rows, width), bf16),
+            in_specs=[pl.BlockSpec(memory_space=pltpu.VMEM)] * 3,
+            out_specs=pl.BlockSpec(memory_space=pltpu.HBM),
+            scratch_shapes=[vmem((chunks, rows, WIDE), bf16), dma((chunks,))],
+            compiler_params=pltpu.CompilerParams(vmem_limit_bytes=16_000_000),
+        )(gated, inverse, gain.reshape(1, -1))
 
     whole = P("seq", "head")
     across = P(None, "head")

time: 29 us -> 28.7 us (0.990)
  local copies, waits for them, and re-layouts: 0.97 us -> 0.01 us
  Pallas kernels: 27.8 us -> 28.6 us
    pallas_call x0 -> x1, Pallas kernels: none -> 1.05 us  [per_device(): pl.pallas_call(scale_kernel, out_shape=jax.ShapeDtypeStruct((rows, width)...]
    unnamed x1 -> x2, local copies, waits for them, and re-layouts: 0.97 us -> 0.01 us
    pallas_call x1, Pallas kernels: 27.8 us -> 27.5 us  [per_device(): pl.pallas_call(functools.partial(kernel, seq_size, head_size), out_shape=...]
where the time goes in v4:
time: 28.7 us; the launch traced here: 28.6 us
  Pallas kernels  28.6 us (100%)
    pallas_call x1, Pallas kernels, per_device(): pl.pallas_call(functools.partial(kernel, seq_size, head_size), out_shape=...  27.5 us
    pallas_call x1, Pallas kernels, per_device(): pl.pallas_call(scale_kernel, out_shape=jax.ShapeDtypeStruct((rows, width)...  1.05 us

profile of v4, /device:TPU:25, one launch (start us, length us, event | category | flops | bytes accessed | tf_op | source)
XLA Modules:
  0.0 28.6 jit_solution(1516036534935973871)
XLA Ops:
  0.0 0.0 copy-start
  0.0 27.5 %shard_map.118 = (f32[8,256,256]{2,1,0:T(8,128)S(1)}, f32[256,128]{1,0:T(8,128)S(1)}) custom-call(s32[4]{0:T(128)} %lengths_hbm.1, bf16[256,2048]{1,0:T(8,128)(2,1)} %xs_hbm.1, bf16[256,2048]{1,0:T(8,128)(2,1)} %z_hbm.1, bf16[256,256]{1,0:T(8,128)(2,1)} %b_hbm.1, bf16[256,256]{1,0:T(8,128)(2,1)} %c_hbm.1, f32[32,256]{1,0:T(8,128)} %bitcast.5, ...), custom_call_target="tpu_custom_call" | custom-call | tf_op jit(solution)/shard_map/pallas_call | solution.py:695
  27.5 0.0 copy-done
  27.5 1.1 %shard_map.119 = bf16[256,2048]{1,0:T(8,128)(2,1)} custom-call(f32[8,256,256]{2,1,0:T(8,128)S(1)} %get-tuple-element.7.gated, f32[256,128]{1,0:T(8,128)S(1)} %get-tuple-element.8.inverse_ref, f32[1,2048]{1,0:T(1,128)S(1)} %bitcast.4), custom_call_target="tpu_custom_call" | custom-call | tf_op jit(solution)/shard_map/pallas_call | solution.py:772
Async XLA Ops:
  0.0 27.5 %copy-start = (f32[2048]{0:T(1024)S(1)}, f32[2048]{0:T(1024)}, u32[]{:S(2)}) copy-start(f32[2048]{0:T(1024)} %param.22) | copy-start | bytes 24580

commit v5 on v4

--- a/solution.py
+++ b/solution.py
@@ -97,7 +97,8 @@
     cum_turned,
     packed,
     hot,
-    hot_wide,
+    cum_columns,
+    carried,
     square,
     square_own,
     square_in,
@@ -139,8 +140,8 @@
 
     def work_chunk(p):
         c = jnp.where(p < 3 * n, p - n, keep + p - 3 * n)
-        c = jnp.where(p < 2 * n, give + p - n, c)
-        return jnp.where(p < n, p, c)
+        early = jnp.where(lax.rem(p, 2) == 0, give + p // 2, p // 2)
+        return jnp.where(p < 2 * n, early, c)
 
     def event_chunk(e):
         c = jnp.where(e < 2 * n, keep + e - n, e - n)
@@ -379,7 +380,6 @@
 
     def hot_step(c, _):
         hot[c] = spread(c, HEAD_DIM)
-        hot_wide[c] = spread(c, BLOCK)
         return 0
 
     lax.fori_loop(0, chunks, hot_step, 0)
@@ -435,22 +435,22 @@
         state = (few[0:1, :] * state0 + state1).astype(bf16)
         own_s[c] = state
 
-        @pl.when((p >= n) & (p < 3 * n))
+        @pl.when((p < 3 * n) & ((p >= 2 * n) | (lax.rem(p, 2) == 0)))
         def _():
             for part in range(NEAR):
-                near_copy(p - n, part).start()
+                near_copy(jnp.where(p < 2 * n, p // 2, p - n), part).start()
 
         @pl.when(p == 0)
         def _():
             d_copy().wait_recv()
 
-        @pl.when((p < n) & (hop == 0) & has_chain_out)
+        @pl.when((p < 2 * n) & (lax.rem(p, 2) != 0) & (hop == 0) & has_chain_out)
         def _():
             decay_pair = dot(d_pair[...], one_hot)[0:1, :]
             wide = state.astype(f32)
-            chain_out[p] = jnp.where(even, decay_pair * wide, wide).astype(bf16)
+            chain_out[p // 2] = jnp.where(even, decay_pair * wide, wide).astype(bf16)
             for part in range(CHAIN):
-                chain_copy(p, part).start()
+                chain_copy(p // 2, part).start()
 
         return 0
 
@@ -461,7 +461,11 @@
 
     packed[2] = split(jnp.concatenate([enters[0], enters[1] * carry0], axis=0))
     packed[3] = split(jnp.concatenate([enters[0], enters[1]], axis=0))
-    packed[4] = split(jnp.concatenate(cums, axis=0))
+    wide = jnp.concatenate(cums, axis=0)
+    wide = jnp.concatenate([wide, jnp.zeros((rows, LANES - heads), f32)], axis=1)
+    for c in range(chunks):
+        shifted = pltpu.roll(wide, LANES - c * per_chunk, 1) if c else wide
+        cum_columns[c] = shifted
     for b in range(blocks):
         wide = jnp.concatenate([cums[b], jnp.zeros((BLOCK, LANES - heads), f32)], axis=1)
         turned = wide.T
@@ -491,18 +495,18 @@
     def local_step(c, _):
         g = c // (chunks // groups)
         one_hot = hot[c]
-        one_hot_wide = hot_wide[c]
         lane = lax.broadcasted_iota(jnp.int32, (BLOCK, LANES), 1)
         locals_ = []
         for b in range(blocks):
             here = slice(b * BLOCK, (b + 1) * BLOCK)
-            across = dot(packed[4, here, :], one_hot_wide)
+            columns = cum_columns[c, here, :]
             damped = score[g, b]
             pieces = []
             for j in range(per_chunk // 2):
                 mixes = []
                 for i in (2 * j, 2 * j + 1):
-                    gap = across[:, i * BLOCK : (i + 1) * BLOCK] - cum_turned[b, c, i : i + 1, :]
+                    across = jnp.broadcast_to(columns[:, i : i + 1], (BLOCK, BLOCK))
+                    gap = across - cum_turned[b, c, i : i + 1, :]
                     mixes.append((damped * jnp.exp(jnp.minimum(gap, 0.0))).astype(bf16))
                 values = scaled[c, here, j * LANES : (j + 1) * LANES]
                 zero = jnp.zeros_like(values)
@@ -515,7 +519,10 @@
         inner = dot(packed[3, BLOCK:, :], one_hot) * dot(c_conv[g, BLOCK:, :], first_s[c])
         few = dot(packed[5, 0:16, :], one_hot)
         total = jnp.concatenate([locals_[0], locals_[1] + inner], axis=0)
-        gated[c] = total + few[8:9, :] * x_conv[c].astype(f32)
+        lanes = pl.ds(pl.multiple_of(c * WIDE, WIDE), WIDE)
+        gate = silu(z_ref[:, lanes].astype(f32))
+        gated[c] = (total + few[8:9, :] * x_conv[c].astype(f32)) * gate
+        carried[c] = dot(packed[2], one_hot) * gate
         return 0
 
     def chain_event(e):
@@ -565,7 +572,7 @@
 
             enter[c, lines] = jnp.where(even, before, middle).astype(bf16)
 
-        @pl.when((e == 2 * n - 1) & (hop == 0))
+        @pl.when((e == events - 1) & (hop == 0))
         def _():
             for other_e in range(2 * n):
                 for part in range(BACK):
@@ -586,9 +593,7 @@
                 back_copy(slot, part).wait_recv()
 
         entering = (enter[c].astype(f32) + back_in[slot].astype(f32)).astype(bf16)
-        total = gated[c] + dot(packed[2], hot[c]) * dot(c_conv[g], entering)
-        lanes = pl.ds(pl.multiple_of(c * WIDE, WIDE), WIDE)
-        value = total * silu(z_ref[:, lanes].astype(f32))
+        value = gated[c] + carried[c] * dot(c_conv[g], entering)
         gated[c] = value
         power = value * value
         square[...] += power[:, :LANES] + power[:, LANES:]
@@ -735,7 +740,8 @@
                 vmem((blocks, chunks, 8, BLOCK), f32),
                 vmem((6, rows, LANES), bf16),
                 vmem((chunks, LANES, WIDE), bf16),
-                vmem((chunks, LANES, per_chunk * BLOCK), bf16),
+                vmem((chunks, rows, LANES), f32),
+                vmem((chunks, rows, WIDE), f32),
                 vmem((rows, LANES), f32),
                 vmem((8, rows), f32),
                 vmem((head_size - 1, 8, rows), f32),

time: 28.7 us -> 28.5 us (level)
  Pallas kernels: 28.6 us -> 28.3 us
where the time goes in v5:
time: 28.5 us; the launch traced here: 28.3 us
  Pallas kernels  28.3 us (99%)
    pallas_call x1, Pallas kernels, per_device(): pl.pallas_call(functools.partial(kernel, seq_size, head_size), out_shape=...  27.3 us
    pallas_call x1, Pallas kernels, per_device(): pl.pallas_call(scale_kernel, out_shape=jax.ShapeDtypeStruct((rows, width)...  1.05 us

profile of v5, /device:TPU:25, one launch (start us, length us, event | category | flops | bytes accessed | tf_op | source)
XLA Modules:
  0.0 28.3 jit_solution(6342959551910972397)
XLA Ops:
  0.0 0.0 copy-start
  0.0 27.3 %shard_map.118 = (f32[8,256,256]{2,1,0:T(8,128)S(1)}, f32[256,128]{1,0:T(8,128)S(1)}) custom-call(s32[4]{0:T(128)} %lengths_hbm.1, bf16[256,2048]{1,0:T(8,128)(2,1)} %xs_hbm.1, bf16[256,2048]{1,0:T(8,128)(2,1)} %z_hbm.1, bf16[256,256]{1,0:T(8,128)(2,1)} %b_hbm.1, bf16[256,256]{1,0:T(8,128)(2,1)} %c_hbm.1, f32[32,256]{1,0:T(8,128)} %bitcast.5, ...), custom_call_target="tpu_custom_call" | custom-call | tf_op jit(solution)/shard_map/pallas_call | solution.py:700
  27.3 0.0 copy-done
  27.3 1.1 %shard_map.119 = bf16[256,2048]{1,0:T(8,128)(2,1)} custom-call(f32[8,256,256]{2,1,0:T(8,128)S(1)} %get-tuple-element.7.gated, f32[256,128]{1,0:T(8,128)S(1)} %get-tuple-element.8.inverse_ref, f32[1,2048]{1,0:T(1,128)S(1)} %bitcast.4), custom_call_target="tpu_custom_call" | custom-call | tf_op jit(solution)/shard_map/pallas_call | solution.py:778
Async XLA Ops:
  0.0 27.3 %copy-start = (f32[2048]{0:T(1024)S(1)}, f32[2048]{0:T(1024)}, u32[]{:S(2)}) copy-start(f32[2048]{0:T(1024)} %param.22) | copy-start | bytes 24580

commit v6 on v5

--- a/solution.py
+++ b/solution.py
@@ -376,7 +376,7 @@
             )
         return 0
 
-    lax.fori_loop(0, 3 * n, conv_step, 0)
+    lax.fori_loop(0, chunks, conv_step, 0)
 
     def hot_step(c, _):
         hot[c] = spread(c, HEAD_DIM)
@@ -455,39 +455,39 @@
         return 0
 
     lax.fori_loop(0, 3 * n, state_step, 0)
-    lax.fori_loop(3 * n, chunks, conv_step, 0)
     lax.fori_loop(3 * n, chunks, state_step, 0)
     load_conv_c.wait()
 
-    packed[2] = split(jnp.concatenate([enters[0], enters[1] * carry0], axis=0))
-    packed[3] = split(jnp.concatenate([enters[0], enters[1]], axis=0))
-    wide = jnp.concatenate(cums, axis=0)
-    wide = jnp.concatenate([wide, jnp.zeros((rows, LANES - heads), f32)], axis=1)
-    for c in range(chunks):
-        shifted = pltpu.roll(wide, LANES - c * per_chunk, 1) if c else wide
-        cum_columns[c] = shifted
-    for b in range(blocks):
-        wide = jnp.concatenate([cums[b], jnp.zeros((BLOCK, LANES - heads), f32)], axis=1)
-        turned = wide.T
+    def prepare():
+        packed[2] = split(jnp.concatenate([enters[0], enters[1] * carry0], axis=0))
+        packed[3] = split(jnp.concatenate([enters[0], enters[1]], axis=0))
+        wide = jnp.concatenate(cums, axis=0)
+        wide = jnp.concatenate([wide, jnp.zeros((rows, LANES - heads), f32)], axis=1)
         for c in range(chunks):
-            cum_turned[b, c, 0:per_chunk, :] = turned[c * per_chunk : (c + 1) * per_chunk, :]
-
-    for g in range(groups):
-        lanes = slice(g * STATE, (g + 1) * STATE)
-        c_conv[g] = convolve(c_ref[:, lanes], conv_c_ref[:, lanes])
-        c_conv[g, 0:HALO, :] = convolve_top(c_ref[0:HALO, lanes], halo_c[:, lanes], conv_c_ref[:, lanes])
-
-    for b in range(blocks):
-        here = slice(b * BLOCK, (b + 1) * BLOCK)
-        allowed = (base + b * BLOCK + s_index >= own_start[here, :]) & (s_index <= t_index)
+            shifted = pltpu.roll(wide, LANES - c * per_chunk, 1) if c else wide
+            cum_columns[c] = shifted
+        for b in range(blocks):
+            wide = jnp.concatenate([cums[b], jnp.zeros((BLOCK, LANES - heads), f32)], axis=1)
+            turned = wide.T
+            for c in range(chunks):
+                cum_turned[b, c, 0:per_chunk, :] = turned[c * per_chunk : (c + 1) * per_chunk, :]
+
         for g in range(groups):
-            value = lax.dot_general(
-                c_conv[g, here, :],
-                b_conv[g, here, :],
-                (((1,), (1,)), ((), ())),
-                preferred_element_type=f32,
-            )
-            score[g, b] = jnp.where(allowed, value, 0.0)
+            lanes = slice(g * STATE, (g + 1) * STATE)
+            c_conv[g] = convolve(c_ref[:, lanes], conv_c_ref[:, lanes])
+            c_conv[g, 0:HALO, :] = convolve_top(c_ref[0:HALO, lanes], halo_c[:, lanes], conv_c_ref[:, lanes])
+
+        for b in range(blocks):
+            here = slice(b * BLOCK, (b + 1) * BLOCK)
+            allowed = (base + b * BLOCK + s_index >= own_start[here, :]) & (s_index <= t_index)
+            for g in range(groups):
+                value = lax.dot_general(
+                    c_conv[g, here, :],
+                    b_conv[g, here, :],
+                    (((1,), (1,)), ((), ())),
+                    preferred_element_type=f32,
+                )
+                score[g, b] = jnp.where(allowed, value, 0.0)
 
     square[...] = jnp.zeros_like(square)
     load_z.wait()
@@ -600,8 +600,8 @@
         return 0
 
     def locals_before(e):
-        count = jnp.where(hop == 0, e - n, chunks)
-        count = jnp.where(hop == 1, e, count)
+        count = jnp.where(hop == 0, jnp.where(e < 2 * n, 0, e - n), chunks)
+        count = jnp.where(hop == 1, jnp.where(e < n, 0, e), count)
         count = jnp.where(hop == 2, e + 3 * n // 2, count)
         count = jnp.where(e >= events, chunks, count)
         return jnp.clip(jnp.where(e < 0, 0, count), 0, chunks)
@@ -612,6 +612,10 @@
         return jnp.where(e >= events, chunks, jnp.minimum(count, chunks))
 
     def outer(e, _):
+        @pl.when(e == jnp.where(hop == 0, 2 * n, jnp.where(hop == 1, n, 0)))
+        def _():
+            prepare()
+
         lax.fori_loop(locals_before(e - 1), locals_before(e), local_step, 0)
 
         @pl.when(e < events)

time: 28.5 us -> 28 us (0.982)
  Pallas kernels: 28.3 us -> 27.8 us
    pallas_call x1, Pallas kernels: 27.3 us -> 26.8 us  [per_device(): pl.pallas_call(functools.partial(kernel, seq_size, head_size), out_shape=...]
where the time goes in v6:
time: 28 us; the launch traced here: 27.9 us
  Pallas kernels  27.8 us (99%)
    pallas_call x1, Pallas kernels, per_device(): pl.pallas_call(functools.partial(kernel, seq_size, head_size), out_shape=...  26.8 us
    pallas_call x1, Pallas kernels, per_device(): pl.pallas_call(scale_kernel, out_shape=jax.ShapeDtypeStruct((rows, width)...  1.05 us

profile of v6, /device:TPU:25, one launch (start us, length us, event | category | flops | bytes accessed | tf_op | source)
XLA Modules:
  0.0 27.9 jit_solution(17663496422678517616)
XLA Ops:
  0.0 0.0 copy-start
  0.0 26.8 %shard_map.118 = (f32[8,256,256]{2,1,0:T(8,128)S(1)}, f32[256,128]{1,0:T(8,128)S(1)}) custom-call(s32[4]{0:T(128)} %lengths_hbm.1, bf16[256,2048]{1,0:T(8,128)(2,1)} %xs_hbm.1, bf16[256,2048]{1,0:T(8,128)(2,1)} %z_hbm.1, bf16[256,256]{1,0:T(8,128)(2,1)} %b_hbm.1, bf16[256,256]{1,0:T(8,128)(2,1)} %c_hbm.1, f32[32,256]{1,0:T(8,128)} %bitcast.5, ...), custom_call_target="tpu_custom_call" | custom-call | tf_op jit(solution)/shard_map/pallas_call | solution.py:704
  26.8 0.0 copy-done
  26.8 1.1 %shard_map.119 = bf16[256,2048]{1,0:T(8,128)(2,1)} custom-call(f32[8,256,256]{2,1,0:T(8,128)S(1)} %get-tuple-element.7.gated, f32[256,128]{1,0:T(8,128)S(1)} %get-tuple-element.8.inverse_ref, f32[1,2048]{1,0:T(1,128)S(1)} %bitcast.4), custom_call_target="tpu_custom_call" | custom-call | tf_op jit(solution)/shard_map/pallas_call | solution.py:782
Async XLA Ops:
  0.0 26.8 %copy-start = (f32[2048]{0:T(1024)S(1)}, f32[2048]{0:T(1024)}, u32[]{:S(2)}) copy-start(f32[2048]{0:T(1024)} %param.22) | copy-start | bytes 24580

commit v7 on v6

--- a/solution.py
+++ b/solution.py
@@ -13,9 +13,9 @@
 LANES = 128
 WIDE = 256
 HALO = 16
-SUBS = 4
+SUBS = 2
 NEAR = 2
-CHAIN = 4
+CHAIN = 2
 BACK = 2
 norm_epsilon = 1e-05
 
@@ -454,8 +454,9 @@
 
         return 0
 
-    lax.fori_loop(0, 3 * n, state_step, 0)
+    lax.fori_loop(0, 2 * n, state_step, 0)
     lax.fori_loop(3 * n, chunks, state_step, 0)
+    lax.fori_loop(2 * n, 3 * n, state_step, 0)
     load_conv_c.wait()
 
     def prepare():

time: 28 us -> 27.8 us (level)
  no operation moved by 1% of the time
where the time goes in v7:
time: 27.8 us; the launch traced here: 27.6 us
  Pallas kernels  27.6 us (99%)
    pallas_call x1, Pallas kernels, per_device(): pl.pallas_call(functools.partial(kernel, seq_size, head_size), out_shape=...  26.6 us
    pallas_call x1, Pallas kernels, per_device(): pl.pallas_call(scale_kernel, out_shape=jax.ShapeDtypeStruct((rows, width)...  1.05 us

profile of v7, /device:TPU:25, one launch (start us, length us, event | category | flops | bytes accessed | tf_op | source)
XLA Modules:
  0.0 27.6 jit_solution(14576136403744215259)
XLA Ops:
  0.0 0.0 copy-start
  0.0 26.6 %shard_map.118 = (f32[8,256,256]{2,1,0:T(8,128)S(1)}, f32[256,128]{1,0:T(8,128)S(1)}) custom-call(s32[4]{0:T(128)} %lengths_hbm.1, bf16[256,2048]{1,0:T(8,128)(2,1)} %xs_hbm.1, bf16[256,2048]{1,0:T(8,128)(2,1)} %z_hbm.1, bf16[256,256]{1,0:T(8,128)(2,1)} %b_hbm.1, bf16[256,256]{1,0:T(8,128)(2,1)} %c_hbm.1, f32[32,256]{1,0:T(8,128)} %bitcast.5, ...), custom_call_target="tpu_custom_call" | custom-call | tf_op jit(solution)/shard_map/pallas_call | solution.py:705
  26.6 0.0 copy-done
  26.6 1.1 %shard_map.119 = bf16[256,2048]{1,0:T(8,128)(2,1)} custom-call(f32[8,256,256]{2,1,0:T(8,128)S(1)} %get-tuple-element.7.gated, f32[256,128]{1,0:T(8,128)S(1)} %get-tuple-element.8.inverse_ref, f32[1,2048]{1,0:T(1,128)S(1)} %bitcast.4), custom_call_target="tpu_custom_call" | custom-call | tf_op jit(solution)/shard_map/pallas_call | solution.py:783
Async XLA Ops:
  0.0 26.6 %copy-start = (f32[2048]{0:T(1024)S(1)}, f32[2048]{0:T(1024)}, u32[]{:S(2)}) copy-start(f32[2048]{0:T(1024)} %param.22) | copy-start | bytes 24580
